TPU v7x, 128 devices: a whole 4x4x4 slice. The times are simulated.
128 devices in a mesh: freq: 8 (over x, core), blk: 16 (over y, z).
Axes of the slice: x: 4, y: 4, z: 4, core: 2. Of those that a mesh axis runs over, the one named last changes fastest.
Arguments:
- sky_maps: bfloat16 [8, 256, 32, 8192], P('freq', 'blk'), may hold values from -24 to 24
- legendre: bfloat16 [128, 256, 4096], P('blk')
- mode_values: int32 [128], replicated, may hold values from 0 to 4095, as said below
- cycle_order: int32 [256], replicated, may hold values from 0 to 255, each once
- bin_widths: int32 [128], replicated, may hold values from 1 to 512, 4096 in all
Outputs:
- cleaned: float32 [32, 2, 128, 4096], P(None, None, None, ('freq', 'blk'))
Inputs may be any that keep to these rules, and one draw needn't show every extreme that they name: Distinct values, 0 and 4095 among them; legendre[s, q, l] is zero wherever l < mode_values[s]. `cycle_order`: each cycle index once.
All inputs are finite; a program needn't handle non-finite values.
Results may differ from a plain program's by a relative error of at most 0.0036.
Values may be sent and summed in bfloat16 or wider, within the bound.
A program may use at most 192 MiB of HBM per device.

v0:
```python
import math

import jax
import jax.numpy as jnp
from jax import lax
from jax.sharding import PartitionSpec as P


def build_trig(mode_values, pixel_count):
    pixels = jnp.arange(pixel_count, dtype=jnp.int32)
    phase_index = pixels[:, None] * mode_values[None, :] % pixel_count
    angles = phase_index.astype(jnp.float32) * jnp.float32(2.0 * math.pi / pixel_count)
    factor = jnp.float32(pixel_count ** (-0.5))
    return (jnp.cos(angles) * factor, -jnp.sin(angles) * factor)


def ilc_weights(spectra):
    chan_count = spectra.shape[1]
    trace_value = jnp.trace(spectra, axis1=1, axis2=2)
    identity = jnp.eye(chan_count, dtype=jnp.float32)
    loaded = (
        spectra
        + (jnp.float32(0.1) * trace_value / jnp.float32(chan_count))[:, None, None] * identity[None]
    )
    lower_factor = jnp.linalg.cholesky(loaded)
    unit_vector = jnp.ones(spectra.shape[:2] + (1,), jnp.float32)
    forward = jax.scipy.linalg.solve_triangular(lower_factor, unit_vector, lower=True)
    solved = jax.scipy.linalg.solve_triangular(lower_factor, forward, trans=1, lower=True)[..., 0]
    return solved / jnp.sum(solved, axis=1, keepdims=True)


def project_mode(left_side, table_rows):
    dims = (((0,), (0,)), ((), ()))
    return lax.dot_general(left_side, table_rows, dims, preferred_element_type=jnp.float32).astype(
        jnp.bfloat16
    )


def clean_band(pieces, ell_start, multiplier, bin_widths):
    chan_count = pieces.shape[0]
    ell_span = pieces.shape[4]
    weighted = pieces * multiplier.astype(jnp.bfloat16)[None, None, None, :, None]
    per_ell = jnp.einsum("ikcsl,jkcsl->ijl", weighted, pieces, preferred_element_type=jnp.float32)
    bin_ends = jnp.cumsum(bin_widths)
    begins = bin_ends - bin_widths
    ell_values = ell_start + jnp.arange(ell_span, dtype=jnp.int32)
    onehot = (
        (ell_values[:, None] >= begins[None, :]) & (ell_values[:, None] < bin_ends[None, :])
    ).astype(jnp.float32)
    partial_value = jnp.dot(
        per_ell.reshape(chan_count * chan_count, ell_span), onehot, precision=lax.Precision.HIGHEST
    )
    spectra = lax.psum(partial_value, ("freq", "blk"))
    weights = ilc_weights(spectra.T.reshape(bin_widths.shape[0], chan_count, chan_count))
    per_ell_weights = jnp.dot(onehot, weights, precision=lax.Precision.HIGHEST)
    return jnp.einsum(
        "ikcsl,li->kcsl",
        pieces.astype(jnp.float32),
        per_ell_weights,
        precision=lax.Precision.HIGHEST,
    )


def on_device(sky_maps, legendre, mode_values, cycle_order, bin_widths):
    groups = lax.axis_size("blk")
    per_device = legendre.shape[0]
    row_count = sky_maps.shape[1]
    map_count = sky_maps.shape[2]
    pixel_count = sky_maps.shape[3]
    ell_count = legendre.shape[2]
    cos_part, sin_part = build_trig(mode_values, pixel_count)
    fourier = jnp.stack(
        [
            cos_part.reshape(pixel_count, groups, per_device),
            sin_part.reshape(pixel_count, groups, per_device),
        ],
        axis=2,
    )
    fourier = fourier.reshape(pixel_count, groups * 2 * per_device).astype(jnp.bfloat16)
    fourier_rows = jnp.dot(
        sky_maps.reshape(row_count * map_count, pixel_count),
        fourier,
        preferred_element_type=jnp.float32,
    )
    fourier_rows = fourier_rows.astype(jnp.bfloat16).reshape(
        row_count, map_count, groups * 2 * per_device
    )
    inverse = jnp.argsort(cycle_order)
    block_index = lax.axis_index("blk")
    freq_index = lax.axis_index("freq")
    multiplier = jnp.where(mode_values > 0, 2.0, 1.0).astype(jnp.float32)
    gathered = lax.all_to_all(fourier_rows, "blk", split_axis=2, concat_axis=0, tiled=True)
    ordered = gathered[inverse]
    item_count = ordered.shape[1]
    results = []
    for slot_index in range(per_device):
        left_side = ordered[:, :, slot_index::per_device].reshape(ordered.shape[0], item_count * 2)
        results.append(project_mode(left_side, legendre[slot_index]))
    stacked = jnp.stack(results, axis=1)
    coeffs = stacked.reshape(item_count, 2, per_device, ell_count)
    pieces = lax.all_to_all(
        lax.all_to_all(coeffs[None], "freq", split_axis=4, concat_axis=0, tiled=True),
        "blk",
        split_axis=4,
        concat_axis=3,
        tiled=True,
    )
    ell_start = (freq_index * groups + block_index) * pieces.shape[4]
    cleaned = clean_band(pieces, ell_start, multiplier, bin_widths)
    return cleaned


def solution(mesh):
    return jax.shard_map(
        on_device,
        mesh=mesh,
        in_specs=(P("freq", "blk", None, None), P("blk", None, None), P(), P(), P()),
        out_specs=P(None, None, None, ("freq", "blk")),
        check_vma=False,
    )
```

profile of v0, /device:TPU:1, one launch (start us, length us, event | category | flops | bytes accessed | tf_op | source)
XLA Modules:
  0.0 697.8 jit_solution(2399682190589871519)
XLA Ops:
  0.7 18.3 %multiply_convert_fusion.1 = (bf16[8192,16,1,8]{0,3,2,1:T(8,128)(2,1)S(1)}, bf16[8192,16,1,8]{0,3,2,1:T(8,128)(2,1)S(1)}) fusion(s32[16,8]{1,0:T(8,128)S(1)} %mul.96), kind=kLoop, calls=%fused_computation.19 | loop fusion | flops 19922944 | bytes 4194816 | tf_op jit(solution)/shard_map/convert
  19.5 3.0 copy-done.3
  22.4 2.4 fusion.22
  27.6 8.6 %all-to-all-start = ((bf16[16,2,4096]{2,1,0:T(2,128)(2,1)}), bf16[16,2,4096]{2,1,0:T(2,128)(2,1)S(1)}, u32[]{:S(2)}, u32[]{:S(2)}) async-start(bf16[16,2,4096]{2,1,0:T(2,128)(2,1)} %reshape.236), calls=%async_computation | async-start | bytes 524288 | tf_op jit(solution)/shard_map/all_to_all | solution.py:92
  36.2 3.2 sort.17
  39.4 4.2 all-to-all-done
  59.3 7.4 %copy.174 = bf16[1,32,2,1,4096]{1,3,2,0,4:T(2,128)(2,1)} copy(bf16[1,32,2,1,4096]{4,2,1,3,0:T(2,128)(2,1)S(1)} %stack.32) | data formatting | bytes 1048576 | tf_op jit(solution)/shard_map/stack | solution.py:99
  69.3 7.4 %copy.175 = bf16[1,32,2,1,4096]{1,3,2,0,4:T(2,128)(2,1)} copy(bf16[1,32,2,1,4096]{4,2,1,3,0:T(2,128)(2,1)S(1)} %stack.33) | data formatting | bytes 1048576 | tf_op jit(solution)/shard_map/stack | solution.py:99
  79.2 7.4 %copy.176 = bf16[1,32,2,1,4096]{1,3,2,0,4:T(2,128)(2,1)} copy(bf16[1,32,2,1,4096]{4,2,1,3,0:T(2,128)(2,1)S(1)} %stack.34) | data formatting | bytes 1048576 | tf_op jit(solution)/shard_map/stack | solution.py:99
  89.2 7.4 %copy.177 = bf16[1,32,2,1,4096]{1,3,2,0,4:T(2,128)(2,1)} copy(bf16[1,32,2,1,4096]{4,2,1,3,0:T(2,128)(2,1)S(1)} %stack.35) | data formatting | bytes 1048576 | tf_op jit(solution)/shard_map/stack | solution.py:99
  99.1 7.4 %copy.178 = bf16[1,32,2,1,4096]{1,3,2,0,4:T(2,128)(2,1)} copy(bf16[1,32,2,1,4096]{4,2,1,3,0:T(2,128)(2,1)S(1)} %stack.36) | data formatting | bytes 1048576 | tf_op jit(solution)/shard_map/stack | solution.py:99
  109.1 7.4 %copy.179 = bf16[1,32,2,1,4096]{1,3,2,0,4:T(2,128)(2,1)} copy(bf16[1,32,2,1,4096]{4,2,1,3,0:T(2,128)(2,1)S(1)} %stack.37) | data formatting | bytes 1048576 | tf_op jit(solution)/shard_map/stack | solution.py:99
  119.0 7.4 %copy.180 = bf16[1,32,2,1,4096]{1,3,2,0,4:T(2,128)(2,1)} copy(bf16[1,32,2,1,4096]{4,2,1,3,0:T(2,128)(2,1)S(1)} %stack.38) | data formatting | bytes 1048576 | tf_op jit(solution)/shard_map/stack | solution.py:99
  128.9 7.4 %copy.181 = bf16[1,32,2,1,4096]{1,3,2,0,4:T(2,128)(2,1)} copy(bf16[1,32,2,1,4096]{4,2,1,3,0:T(2,128)(2,1)S(1)} %stack.39) | data formatting | bytes 1048576 | tf_op jit(solution)/shard_map/stack | solution.py:99
  136.3 85.4 %stack.40 = bf16[1,32,2,8,4096]{1,3,2,0,4:T(8,128)(2,1)} concatenate(bf16[1,32,2,1,4096]{1,3,2,0,4:T(2,128)(2,1)} %copy.174, bf16[1,32,2,1,4096]{1,3,2,0,4:T(2,128)(2,1)} %copy.175, bf16[1,32,2,1,4096]{1,3,2,0,4:T(2,128)(2,1)} %copy.176, bf16[1,32,2,1,4096]{1,3,2,0,4:T(2,128)(2,1)} %copy.177, bf16[1,32,2,1,4096]{1,3,2,0,4:T(2,128)(2,1)} %copy.178, ...), dimensions={3} | concatenate | bytes 8388608 | tf_op jit(solution)/shard_map/stack | solution.py:99
  221.7 18.9 %reshape.238 = bf16[8,2,131072]{2,1,0:T(2,128)(2,1)} reshape(bf16[4096,1,2,8,32]{4,3,2,1,0:T(8,128)(2,1)} %bitcast.108) | data formatting | bytes 8388608
  240.6 55.1 %all_to_all.54 = bf16[8,2,131072]{2,1,0:T(2,128)(2,1)} all-to-all(bf16[8,2,131072]{2,1,0:T(2,128)(2,1)} %reshape.238), channel_id=1, replica_groups=mesh['freq'=8,'blk'=16] {'freq'}, dimensions={0} | all-to-all | bytes 8388608 | tf_op jit(solution)/shard_map/all_to_all | solution.py:102
  295.7 12.4 %reshape.239 = bf16[4096,1,2,8,32]{4,3,2,1,0:T(8,128)(2,1)} reshape(bf16[8,2,131072]{2,1,0:T(2,128)(2,1)} %all_to_all.54) | data formatting | bytes 8388608
  308.2 15.3 %copy.218 = bf16[8,32,2,8,512]{1,3,2,0,4:T(8,128)(2,1)} copy(bf16[8,32,2,8,512]{1,3,2,4,0:T(8,128)(2,1)} %bitcast.109) | data formatting | bytes 8388608 | tf_op jit(solution)/shard_map/all_to_all | solution.py:102
  323.5 20.8 %reshape.240 = bf16[16,2,65536]{2,1,0:T(2,128)(2,1)} reshape(bf16[512,8,2,8,32]{4,3,2,1,0:T(8,128)(2,1)} %bitcast.110) | data formatting | bytes 8388608
  344.2 4.7 all-to-all-start.2
  349.5 59.1 %all-to-all-done.2 = bf16[16,2,65536]{2,1,0:T(2,128)(2,1)} async-done(((bf16[16,2,65536]{2,1,0:T(2,128)(2,1)}), bf16[16,2,65536]{2,1,0:T(2,128)(2,1)}, u32[]{:S(2)}, u32[]{:S(2)}) %all-to-all-start.2) | async-done | bytes 4194336 | tf_op jit(solution)/shard_map/all_to_all | solution.py:101
  408.6 16.0 %reshape.241 = bf16[512,8,2,8,32]{4,3,2,1,0:T(8,128)(2,1)} reshape(bf16[16,2,65536]{2,1,0:T(2,128)(2,1)} %all-to-all-done.2) | data formatting | bytes 8388608
  424.6 36.1 %copy.185 = bf16[8,32,2,16,8,32]{5,4,3,2,1,0:T(8,128)(2,1)} copy(bf16[8,32,2,16,8,32]{1,4,2,0,5,3:T(8,128)(2,1)} %bitcast.111) | data formatting | bytes 8388608 | tf_op jit(solution)/shard_map/all_to_all | solution.py:101
  460.7 14.3 %broadcast_multiply_fusion = bf16[8,32,2,128,32]{4,3,2,1,0:T(8,128)(2,1)} fusion(bf16[128]{0:T(256)(128)(2,1)S(1)} %fusion.35, bf16[8,32,2,16,8,32]{5,4,3,2,1,0:T(8,128)(2,1)} %copy.185), kind=kLoop, calls=%fused_computation.2 | loop fusion | flops 2097152 | bytes 8388864 | tf_op jit(solution)/shard_map/mul | solution.py:42
  475.0 16.1 %copy.187 = bf16[8,32,2,128,32]{3,0,1,2,4:T(8,128)(2,1)} copy(bf16[8,32,2,128,32]{4,3,2,1,0:T(8,128)(2,1)} %broadcast_multiply_fusion) | data formatting | bytes 8388608 | tf_op jit(solution)/shard_map/mul | solution.py:42
  491.1 16.0 %copy.186 = bf16[8,32,2,128,32]{3,0,1,2,4:T(8,128)(2,1)} copy(bf16[8,32,2,128,32]{4,3,2,1,0:T(8,128)(2,1)} %bitcast.107) | data formatting | bytes 8388608 | tf_op jit(solution)/shard_map/all_to_all | solution.py:101
  507.1 6.3 convolution_bitcast_fusion
  513.7 70.2 %psum.7 = f32[128,64]{0,1:T(8,128)S(1)} all-reduce(f32[128,64]{0,1:T(8,128)S(1)} %fusion.23), channel_id=1, replica_groups=mesh['freq'=8,'blk'=16] {'freq','blk'}, use_global_device_ids=true, to_apply=%region_2.3 | all-reduce | flops 8192 | bytes 65536 | tf_op jit(solution)/shard_map/psum | solution.py:53
  584.4 93.9 %custom-call.11 = f32[128,8,8]{2,1,0:T(8,128)S(1)} custom-call(f32[128,8,8]{2,1,0:T(8,128)S(1)} %broadcast_multiply_fusion.1), custom_call_target="Cholesky" | custom-call | tf_op jit(solution)/shard_map/jit(cholesky)/cholesky | solution.py:25
  681.0 13.2 %multiply_reduce_fusion = f32[32,32,2,128]{0,3,2,1:T(8,128)} fusion(f32[32,8]{0,1:T(8,128)S(1)} %fusion.25, bf16[8,32,2,16,8,32]{5,4,3,2,1,0:T(8,128)(2,1)} %copy.185), kind=kLoop, calls=%fused_computation.1 | loop fusion | flops 6029312 | bytes 5243904
  694.2 3.6 copy.207
  (88 shorter events, 41.1 us)
Async XLA Ops:
  19.1 3.4 copy-start.3
  22.4 13.8 %copy-start = (s32[256]{0:T(256)S(1)}, s32[256]{0:T(256)}, u32[]{:S(2)}) copy-start(s32[256]{0:T(256)} %param.8) | copy-start | bytes 3076
  27.6 16.1 %all-to-all-start = ((bf16[16,2,4096]{2,1,0:T(2,128)(2,1)}), bf16[16,2,4096]{2,1,0:T(2,128)(2,1)S(1)}, u32[]{:S(2)}, u32[]{:S(2)}) async-start(bf16[16,2,4096]{2,1,0:T(2,128)(2,1)} %reshape.236), calls=%async_computation | async-start | bytes 524288 | tf_op jit(solution)/shard_map/all_to_all | solution.py:92
  344.2 4.7 copy-start.1
  344.2 5.2 copy-start.2
  344.2 64.3 %all-to-all-start.2 = ((bf16[16,2,65536]{2,1,0:T(2,128)(2,1)}), bf16[16,2,65536]{2,1,0:T(2,128)(2,1)}, u32[]{:S(2)}, u32[]{:S(2)}) async-start(bf16[16,2,65536]{2,1,0:T(2,128)(2,1)} %reshape.240), calls=%async_computation.2 | async-start | bytes 8388608 | tf_op jit(solution)/shard_map/all_to_all | solution.py:101
where the time goes:
time: 711 us; the launch traced here: 698 us
  local copies, waits for them, and re-layouts  324 us (46%)
  other arithmetic  145 us (20%)
  blocking collectives  125 us (18%)
  waiting for transfers between devices  63.3 us (9%)
  matrix products  26.6 us (4%)
  starting transfers between devices  13.3 us (2%)
    another operation x17, local copies, waits for them, and re-layouts, on_device(): stacked = jnp.stack(results, axis=1)  147 us
    another operation x4, other arithmetic, ilc_weights(): lower_factor = jnp.linalg.cholesky(loaded)  94.1 us
    unnamed x15, local copies, waits for them, and re-layouts  73.4 us
    psum x1, blocking collectives, clean_band(): spectra = lax.psum(partial_value, ('freq', 'blk'))  70.2 us
    all_to_all x1, waiting for transfers between devices, on_device(): lax.all_to_all(lax.all_to_all(coeffs[None], 'freq', split_axis=4, concat_...  59.1 us
    all_to_all x1, blocking collectives, on_device(): lax.all_to_all(coeffs[None], 'freq', split_axis=4, concat_axis=0, tiled=T...  55.1 us
    all_to_all x2, local copies, waits for them, and re-layouts, on_device(): lax.all_to_all(lax.all_to_all(coeffs[None], 'freq', split_axis=4, concat_...  52.1 us
    another operation x3, other arithmetic  18.6 us
  transfers between devices with their start and end apart: 2, of which 2 were waited for; matrix products, arithmetic and copies ran while one was open for 1% of the time, Pallas kernels for 0%

commit v1 on v0

v1 whole, which is shorter than its diff:
```python
import functools
import math

import jax
import jax.numpy as jnp
from jax import lax
from jax.experimental import pallas as pl
from jax.experimental.pallas import tpu as pltpu
from jax.sharding import PartitionSpec as P

F32 = jnp.float32
BF16 = jnp.bfloat16
PIX = 8192
PAIRS = [(i, j) for i in range(8) for j in range(i, 8)]
PROWS = 40
MESH = pl.DeviceIdType.MESH
VMEM = pltpu.VMEM
DMA = pltpu.SemaphoreType.DMA


def vspec():
    return pl.BlockSpec(memory_space=pltpu.VMEM)


def split_dot(a, b, dims):
    hi = a.astype(BF16)
    rest = a - hi.astype(F32)
    mid = rest.astype(BF16)
    low = (rest - mid.astype(F32)).astype(BF16)
    out = lax.dot_general(low, b, dims, preferred_element_type=F32)
    out += lax.dot_general(mid, b, dims, preferred_element_type=F32)
    return out + lax.dot_general(hi, b, dims, preferred_element_type=F32)


NN = (((1,), (0,)), ((), ()))
NT = (((1,), (1,)), ((), ()))


def swap_blocks(arrays, width):
    count = len(arrays)
    block = lax.broadcasted_iota(jnp.int32, arrays[0].shape, 1) // width
    arrays = list(arrays)
    step = 1
    while step < count:
        low = (block // step) % 2 == 0
        for i in range(count):
            if i & step:
                continue
            a, b = arrays[i], arrays[i | step]
            arrays[i] = jnp.where(low, a, pltpu.roll(b, step * width, 1))
            arrays[i | step] = jnp.where(low, pltpu.roll(a, 128 - step * width, 1), b)
        step *= 2
    return arrays


CHUNKS = 16


def sky_copy(x_hbm, xbuf, sem, n):
    width = PIX // CHUNKS
    return pltpu.make_async_copy(
        x_hbm.at[:, pl.ds(pl.multiple_of(n * width, width), width)], xbuf.at[n], sem.at[n]
    )


def fourier_part(m_ref, x_hbm, sb_ref, xbuf, tab_a, tab_b, rows, sem):
    lax.fori_loop(0, CHUNKS, lambda n, _: (sky_copy(x_hbm, xbuf, sem, n).start(), 0)[1], 0)
    m = m_ref[...]
    step = jnp.float32(2.0 * math.pi / PIX)
    high = lax.broadcasted_iota(jnp.int32, (64, 256), 0)
    quarter = (lax.broadcasted_iota(jnp.int32, (64, 256), 1) // 8) % 2 * (PIX // 4)
    ang = (((high * m) % 64 * 128 + quarter) % PIX).astype(F32) * step
    factor = jnp.float32(PIX ** (-0.5))
    tab_a[0] = jnp.cos(ang) * factor
    tab_a[1] = jnp.sin(ang) * factor
    low = lax.broadcasted_iota(jnp.int32, (128, 256), 0)
    ang = ((low * m) % PIX).astype(F32) * step
    tab_b[0] = jnp.cos(ang)
    tab_b[1] = jnp.sin(ang)
    rows[...] = jnp.zeros_like(rows)

    def chunk(n, _):
        parts = []
        for u in range(4):
            ca = tab_a[0, pl.ds(n * 4 + u, 1), :]
            sa = tab_a[1, pl.ds(n * 4 + u, 1), :]
            parts.append((tab_b[0] * ca - tab_b[1] * sa).astype(BF16))
        table = jnp.concatenate(parts, axis=0)
        sky_copy(x_hbm, xbuf, sem, n).wait()
        out = jnp.dot(xbuf[n], table, preferred_element_type=F32)
        rows[0] += out[:, :128]
        rows[1] += out[:, 128:]
        return 0

    lax.fori_loop(0, CHUNKS, chunk, 0)

    for xg in range(4):
        for half in range(2):
            parts = [rows[half, pl.ds(xg * 8 + k, 16, stride=32), :] for k in range(8)]
            for g, part in enumerate(swap_blocks(parts, 16)):
                sb_ref[xg, half * 8 + g] = part.astype(BF16)


def fourier_kernel(m_ref, x_hbm, sb_ref, xbuf, tab_a, tab_b, rows, sem):
    fourier_part(m_ref, x_hbm, sb_ref, xbuf, tab_a, tab_b, rows, sem)


def fourier_call(mcol, sky):
    return pl.pallas_call(
        fourier_kernel,
        out_shape=jax.ShapeDtypeStruct((4, 16, 16, 128), BF16),
        in_specs=[vspec(), pl.BlockSpec(memory_space=pl.ANY)],
        out_specs=vspec(),
        scratch_shapes=[
            VMEM((CHUNKS, 512, PIX // CHUNKS), BF16),
            VMEM((2, 64, 256), F32),
            VMEM((2, 128, 256), F32),
            VMEM((2, 512, 128), F32),
            DMA((CHUNKS,)),
        ],
        compiler_params=pltpu.CompilerParams(vmem_limit_bytes=32 << 20),
        name="fourier",
    )(mcol, sky)


def place():
    freq = lax.axis_index("freq")
    blk = lax.axis_index("blk")
    return freq // 2, freq % 2, blk


def greet(peers):
    barrier = pltpu.get_barrier_semaphore()
    total = 0
    for count, peer in peers:
        total += count

        def one(d, _, peer=peer):
            pl.semaphore_signal(barrier, inc=1, device_id=peer(d), device_id_type=MESH)
            return 0

        lax.fori_loop(1, count + 1, one, 0)
    pl.semaphore_wait(barrier, total)


def plane_peer(x, c, b, d):
    q = (x * 16 + b + d) % 64
    return (q // 16 * 2 + c, q % 16)


def plane_copy(src, dst, send, recv, x, c, b, d):
    q = (x * 16 + b + d) % 64
    return pltpu.make_async_remote_copy(
        src_ref=src.at[q // 16, q % 16],
        dst_ref=dst.at[x, b],
        send_sem=send.at[d],
        recv_sem=recv.at[x * 16 + b],
        device_id=(q // 16 * 2 + c, q % 16),
        device_id_type=MESH,
    )


def plane_arrival(src, dst, send, recv, x, c, b, p):
    return pltpu.make_async_remote_copy(
        src_ref=src.at[p // 16, p % 16],
        dst_ref=dst.at[p // 16, p % 16],
        send_sem=send.at[0],
        recv_sem=recv.at[p],
        device_id=(x * 2 + c, b),
        device_id_type=MESH,
    )


def plane_start(src, dst, send, recv, own, x, c, b):
    pltpu.make_async_copy(src.at[x, b], dst.at[x, b], own).start()

    def one(d, _):
        plane_copy(src, dst, send, recv, x, c, b, d).start()
        return 0

    lax.fori_loop(1, 64, one, 0)


def plane_send_wait(src, dst, send, recv, x, c, b):
    def one(d, _):
        plane_copy(src, dst, send, recv, x, c, b, d).wait_send()
        return 0

    lax.fori_loop(1, 64, one, 0)


def modes_exchange(sb_ref, rb_ref, send, recv, own, fsend, frecv):
    x, c, b = place()
    mine = rb_ref.at[c]
    theirs = rb_ref.at[1 - c]
    plane_start(sb_ref, mine, send, recv, own, x, c, b)
    pltpu.make_async_copy(sb_ref.at[x, b], mine.at[x, b], own).wait()

    def forward(g):
        return pltpu.make_async_remote_copy(
            src_ref=mine.at[g],
            dst_ref=mine.at[g],
            send_sem=fsend.at[g],
            recv_sem=frecv.at[g],
            device_id=(x * 2 + 1 - c, b),
            device_id_type=MESH,
        )

    def group(i, _):
        g = (x + i) % 4

        def one(j, _):
            p = g * 16 + j

            @pl.when(p != x * 16 + b)
            def _():
                plane_arrival(sb_ref, mine, send, recv, x, c, b, p).wait_recv()

            return 0

        lax.fori_loop(0, 16, one, 0)
        forward(g).start()
        return 0

    lax.fori_loop(0, 4, group, 0)
    plane_send_wait(sb_ref, mine, send, recv, x, c, b)

    def finish(g, _):
        forward(g).wait_send()
        pltpu.make_async_remote_copy(
            src_ref=theirs.at[g],
            dst_ref=theirs.at[g],
            send_sem=fsend.at[g],
            recv_sem=frecv.at[g],
            device_id=(x * 2 + 1 - c, b),
            device_id_type=MESH,
        ).wait_recv()
        return 0

    lax.fori_loop(0, 4, finish, 0)


def modes_kernel(sb_ref, rb_ref, send, recv, own, fsend, frecv):
    x, c, b = place()
    greet([
        (63, lambda d: plane_peer(x, c, b, d)),
        (1, lambda d: (x * 2 + 1 - c, b)),
    ])
    modes_exchange(sb_ref, rb_ref, send, recv, own, fsend, frecv)


def modes_call(sb):
    return pl.pallas_call(
        modes_kernel,
        out_shape=jax.ShapeDtypeStruct((2, 4, 16, 16, 128), BF16),
        in_specs=[vspec()],
        out_specs=vspec(),
        scratch_shapes=[DMA((64,)), DMA((64,)), DMA, DMA((4,)), DMA((4,))],
        compiler_params=pltpu.CompilerParams(collective_id=0, has_side_effects=True),
        name="modes_exchange",
    )(sb)


def sum_over_devices(part, got, send, recv):
    x, c, b = place()
    y, z = b // 4, b % 4
    stages = [
        (3, lambda d: (x * 2 + c, y * 4 + (z + d) % 4)),
        (3, lambda d: (x * 2 + c, (y + d) % 4 * 4 + z)),
        (3, lambda d: ((x + d) % 4 * 2 + c, b)),
        (1, lambda d: (x * 2 + 1 - c, b)),
    ]
    base = 0
    for index, (count, peer) in enumerate(stages):
        copies = []
        for d in range(1, count + 1):
            copies.append(
                pltpu.make_async_remote_copy(
                    src_ref=part.at[index],
                    dst_ref=got.at[base + d - 1],
                    send_sem=send.at[base + d - 1],
                    recv_sem=recv.at[base + d - 1],
                    device_id=peer(d),
                    device_id_type=MESH,
                )
            )
        for copy in copies:
            copy.start()
        total = part[index]
        for d, copy in enumerate(copies):
            copy.wait_recv()
            total = total + got[base + d]
        part[index + 1] = total
        for copy in copies:
            copy.wait_send()
        base += count


def sum_peers():
    x, c, b = place()
    y, z = b // 4, b % 4
    return [
        (3, lambda d: (x * 2 + c, y * 4 + (z + d) % 4)),
        (3, lambda d: (x * 2 + c, (y + d) % 4 * 4 + z)),
        (3, lambda d: ((x + d) % 4 * 2 + c, b)),
        (1, lambda d: (x * 2 + 1 - c, b)),
    ]


def solve_bins(packed, matrix):
    for row, (i, j) in enumerate(PAIRS):
        value = packed[pl.ds(row, 1), :]
        matrix[j, pl.ds(i, 1), :] = value
        if i != j:
            matrix[i, pl.ds(j, 1), :] = value
    columns = [matrix[j] for j in range(8)]
    rows = lax.broadcasted_iota(jnp.int32, (8, 128), 0)
    trace = sum(columns[j][j : j + 1] for j in range(8))
    load = jnp.float32(0.1) * trace / jnp.float32(8)
    columns = [columns[j] + jnp.where(rows == j, load, 0.0) for j in range(8)]
    z = jnp.ones((8, 128), F32)
    for j in range(8):
        pivot = columns[j][j : j + 1]
        scale = columns[j] / pivot
        keep = rows == j
        for k in range(j + 1, 8):
            columns[k] = columns[k] - jnp.where(keep, 0.0, scale * columns[k][j : j + 1])
        z = z - jnp.where(keep, 0.0, scale * z[j : j + 1])
        columns[j] = jnp.where(keep, columns[j], 0.0)
    diagonal = sum(columns)
    z = z / diagonal
    return z / jnp.sum(z, axis=0, keepdims=True)


def weights_kernel(sp_ref, w_ref, part, got, matrix, send, recv):
    greet(sum_peers())
    part[0] = sp_ref[...]
    sum_over_devices(part, got, send, recv)
    w_ref[...] = solve_bins(part.at[4], matrix)


def weights_call(sp):
    return pl.pallas_call(
        weights_kernel,
        out_shape=jax.ShapeDtypeStruct((8, 128), F32),
        in_specs=[vspec()],
        out_specs=vspec(),
        scratch_shapes=[
            VMEM((5, PROWS, 128), F32),
            VMEM((10, PROWS, 128), F32),
            VMEM((8, 8, 128), F32),
            DMA((10,)),
            DMA((10,)),
        ],
        compiler_params=pltpu.CompilerParams(collective_id=1, has_side_effects=True),
        name="weights",
    )(sp)


def bands_kernel(sb_ref, rb_ref, send, recv, own):
    x, c, b = place()
    greet([(63, lambda d: plane_peer(x, c, b, d))])
    plane_start(sb_ref, rb_ref, send, recv, own, x, c, b)
    pltpu.make_async_copy(sb_ref.at[x, b], rb_ref.at[x, b], own).wait()

    def one(d, _):
        p = (x * 16 + b + 64 - d) % 64
        plane_arrival(sb_ref, rb_ref, send, recv, x, c, b, p).wait_recv()
        return 0

    lax.fori_loop(1, 64, one, 0)
    plane_send_wait(sb_ref, rb_ref, send, recv, x, c, b)


def bands_call(sb):
    return pl.pallas_call(
        bands_kernel,
        out_shape=jax.ShapeDtypeStruct((4, 16, 32, 128), BF16),
        in_specs=[vspec()],
        out_specs=vspec(),
        scratch_shapes=[DMA((64,)), DMA((64,)), DMA],
        compiler_params=pltpu.CompilerParams(collective_id=2, has_side_effects=True),
        name="bands_exchange",
    )(sb)


def legendre_copy(leg_hbm, leg, sem, c, i):
    start = pl.multiple_of((i % 4 * 2 + c) * 512, 512)
    return pltpu.make_async_copy(
        leg_hbm.at[i // 4, :, pl.ds(start, 512)], leg.at[i // 4, i % 4], sem.at[i]
    )


def bin_rows(widths_ref, c, onehot):
    row = lax.broadcasted_iota(jnp.int32, (128, 128), 0)
    col = lax.broadcasted_iota(jnp.int32, (128, 128), 1)
    upper = jnp.where(row <= col, 1.0, 0.0).astype(BF16)
    widths = widths_ref[...].astype(F32)
    ends = split_dot(widths, upper, NN)
    begins = ends - widths
    ends, begins = ends[0:1], begins[0:1]

    def chunk(g, _):
        ell = lax.broadcasted_iota(jnp.int32, (512, 128), 0) + ((g * 2 + c) * 512)
        ell = ell.astype(F32)
        hit = jnp.where(ell >= begins, 1.0, 0.0) * jnp.where(ell < ends, 1.0, 0.0)
        onehot[pl.ds(pl.multiple_of(g * 512, 512), 512), :] = hit.astype(BF16)
        return 0

    lax.fori_loop(0, 4, chunk, 0)


def order_rows(rb, order_ref, left, turned):
    q = lax.broadcasted_iota(jnp.int32, (256, 256), 0)
    perm = jnp.where(q == order_ref[...], 1.0, 0.0).astype(BF16)

    def channel(ch, _):
        block = rb[ch % 2, ch // 2]
        sorted_rows = jnp.dot(perm, block, preferred_element_type=F32)
        for h in range(2):
            turned[h] = sorted_rows[h * 128 : h * 128 + 128].T
            for s in range(8):
                left[s, pl.ds(pl.multiple_of(ch * 16, 16), 16), h * 128 : h * 128 + 128] = turned[
                    h, pl.ds(s, 16, stride=8), :
                ].astype(BF16)
        return 0

    lax.fori_loop(0, 8, channel, 0)


def legendre_sums(leg_hbm, leg, sem, c, left, coef):
    def one(i, _):
        legendre_copy(leg_hbm, leg, sem, c, i).wait()
        out = jnp.dot(left[i // 4], leg[i // 4, i % 4], preferred_element_type=F32)
        coef[i // 4, :, pl.ds(pl.multiple_of(i % 4 * 512, 512), 512)] = out.astype(BF16)
        return 0

    lax.fori_loop(0, 32, one, 0)


def cross_spectra(coef, mult, sums, per_ell):
    def tile(t, _):
        lanes = pl.ds(pl.multiple_of(t * 128, 128), 128)
        acc = [jnp.zeros((8, 128), F32) for _ in PAIRS]

        def slot(s, acc):
            acc = list(acc)
            for half in range(1):
                values = [coef[s, i * 16 : i * 16 + 16, lanes].astype(F32) for i in range(8)]
                factor = mult(s)
                scaled = [v * factor for v in values]
                for n, (i, j) in enumerate(PAIRS):
                    prod = scaled[i] * values[j]
                    acc[n] = acc[n] + (prod[0:8] + prod[8:16])
            return tuple(acc)

        acc = lax.fori_loop(0, 8, slot, tuple(acc))
        for n, value in enumerate(acc):
            sums[n * 8 : n * 8 + 8, :] = value
        total = sums[pl.ds(0, PROWS, stride=8), :]
        for r in range(1, 8):
            total = total + sums[pl.ds(r, PROWS, stride=8), :]
        per_ell[:, lanes] = total
        return 0

    sums[...] = jnp.zeros_like(sums)
    lax.fori_loop(0, 16, tile, 0)


def slot_mult(mv_ref, b):
    return lambda s: (1 + jnp.minimum(mv_ref[b * 8 + s], 1)).astype(F32)


def spectra_kernel(mv_ref, order_ref, widths_ref, rb_ref, leg_hbm, coef_ref, sp_ref, onehot_ref, leg, left, turned, sums, per_ell, sem):
    x, c, b = place()
    lax.fori_loop(0, 32, lambda i, _: (legendre_copy(leg_hbm, leg, sem, c, i).start(), 0)[1], 0)
    bin_rows(widths_ref, c, onehot_ref)
    order_rows(rb_ref, order_ref, left, turned)
    legendre_sums(leg_hbm, leg, sem, c, left, coef_ref)
    cross_spectra(coef_ref, slot_mult(mv_ref, b), sums, per_ell)
    sp_ref[...] = split_dot(per_ell[...], onehot_ref[...], NN)


def spectra_call(mv, order, widths, rb, leg):
    return pl.pallas_call(
        spectra_kernel,
        out_shape=(
            jax.ShapeDtypeStruct((8, 128, 2048), BF16),
            jax.ShapeDtypeStruct((PROWS, 128), F32),
            jax.ShapeDtypeStruct((2048, 128), BF16),
        ),
        in_specs=[
            pl.BlockSpec(memory_space=pltpu.SMEM),
            vspec(),
            vspec(),
            vspec(),
            pl.BlockSpec(memory_space=pl.ANY),
        ],
        out_specs=(vspec(), vspec(), vspec()),
        scratch_shapes=[
            VMEM((8, 4, 256, 512), BF16),
            VMEM((8, 128, 256), BF16),
            VMEM((2, 128, 128), F32),
            VMEM((PROWS * 8, 128), F32),
            VMEM((PROWS, 2048), F32),
            DMA((32,)),
        ],
        compiler_params=pltpu.CompilerParams(vmem_limit_bytes=40 << 20),
        name="spectra",
    )(mv, order, widths, rb, leg)


def weighted_sums(coef, weights, onehot, table, turned, sb):
    table[...] = split_dot(weights, onehot[...], NT)

    def tile(t, _):
        lanes = pl.ds(pl.multiple_of(t * 128, 128), 128)
        per = [jnp.broadcast_to(table[i : i + 1, lanes], (16, 128)) for i in range(8)]
        for s in range(8):
            total = per[0] * coef[s, 0:16, lanes].astype(F32)
            for i in range(1, 8):
                total += per[i] * coef[s, i * 16 : i * 16 + 16, lanes].astype(F32)
            turned[pl.ds(s, 16, stride=8), :] = total
        out = turned[...].T.astype(BF16)
        for j in range(4):
            sb[t // 4, t % 4 * 4 + j] = out[j * 32 : j * 32 + 32]
        return 0

    lax.fori_loop(0, 16, tile, 0)


def clean_kernel(w_ref, onehot_ref, coef_ref, sb_ref, table, turned):
    weighted_sums(coef_ref, w_ref[...], onehot_ref, table, turned, sb_ref)


def clean_call(weights, onehot, coef):
    return pl.pallas_call(
        clean_kernel,
        out_shape=jax.ShapeDtypeStruct((4, 16, 32, 128), BF16),
        in_specs=[vspec(), vspec(), vspec()],
        out_specs=vspec(),
        scratch_shapes=[VMEM((8, 2048), F32), VMEM((128, 128), F32)],
        compiler_params=pltpu.CompilerParams(vmem_limit_bytes=32 << 20),
        name="weighted_sums",
    )(weights, onehot, coef)


def layout_kernel(rb_ref, out_ref):
    def group(i, _):
        x, rows = i // 4, pl.ds(pl.multiple_of(i % 4 * 8, 8), 8)
        parts = [rb_ref[x, b, rows, :].astype(F32) for b in range(16)]
        for kc, part in enumerate(swap_blocks(parts, 8)):
            out_ref[x * 16 + kc, rows, :] = part
        return 0

    lax.fori_loop(0, 16, group, 0)


def layout_call(rb):
    return pl.pallas_call(
        layout_kernel,
        out_shape=jax.ShapeDtypeStruct((64, 32, 128), F32),
        in_specs=[vspec()],
        out_specs=vspec(),
        name="output_layout",
    )(rb)


def on_device(sky_maps, legendre, mode_values, cycle_order, bin_widths):
    sky = sky_maps.reshape(512, PIX)
    slots = mode_values.reshape(16, 1, 8)
    mcol = jnp.broadcast_to(slots, (16, 2, 8)).reshape(1, 256)
    order = cycle_order.reshape(1, 256)
    widths = jnp.broadcast_to(bin_widths.reshape(1, 128), (8, 128))
    sb = fourier_call(mcol, sky)
    rb = modes_call(sb).reshape(2, 4, 256, 128)
    coef, sp, onehot = spectra_call(mode_values, order, widths, rb, legendre)
    weights = weights_call(sp)
    sb = clean_call(weights, onehot, coef)
    out = layout_call(bands_call(sb))
    return out.reshape(32, 2, 32, 128).transpose(0, 1, 3, 2)


def solution(mesh):
    return jax.shard_map(
        on_device,
        mesh=mesh,
        in_specs=(P("freq", "blk", None, None), P("blk", None, None), P(), P(), P()),
        out_specs=P(None, None, None, ("freq", "blk")),
        check_vma=False,
    )
```

time: 711 us -> 103 us (0.14); the launches traced: 698 us -> 101 us
  local copies, waits for them, and re-layouts: 324 us -> 12.8 us
  other arithmetic: 145 us -> 0 us
  blocking collectives: 125 us -> 0 us
  Pallas kernels: 0 us -> 88.4 us
  waiting for transfers between devices: 63.3 us -> 0 us
  matrix products: 26.6 us -> 0 us
  starting transfers between devices: 13.3 us -> 0 us
    another operation x22 -> x0, local copies, waits for them, and re-layouts: 148 us -> none  [the longest x17 147 us: on_device(): stacked = jnp.stack(results, axis=1)]
    another operation x12 -> x0, other arithmetic: 114 us -> none  [the longest x4 94.1 us: ilc_weights(): lower_factor = jnp.linalg.cholesky(loaded)]
    pallas_call x0 -> x7, Pallas kernels: none -> 88.4 us  [the longest x1 20.6 us: modes_call(): pl.pallas_call(modes_kernel, out_shape=jax.ShapeDtypeStruct((2, 4, 16, 16...]
    psum x1 -> x0, blocking collectives: 70.2 us -> none  [clean_band(): spectra = lax.psum(partial_value, ('freq', 'blk'))]
    all_to_all x4 -> x0, local copies, waits for them, and re-layouts: 67.7 us -> none  [the longest x2 52.1 us: on_device(): lax.all_to_all(lax.all_to_all(coeffs[None], 'freq', split_axis=4, concat_...]
    all_to_all x2 -> x0, waiting for transfers between devices: 63.3 us -> none  [the longest x1 59.1 us: on_device(): lax.all_to_all(lax.all_to_all(coeffs[None], 'freq', split_axis=4, concat_...]
    unnamed x15 -> x20, local copies, waits for them, and re-layouts: 73.4 us -> 11.3 us
    all_to_all x1 -> x0, blocking collectives: 55.1 us -> none  [on_device(): lax.all_to_all(coeffs[None], 'freq', split_axis=4, concat_axis=0, tiled=T...]
  transfers between devices with their start and end apart: 2 -> 0, of which waited for: 2 -> 0; matrix products, arithmetic and copies ran while one was open for 1% -> 0% of each run, Pallas kernels for 0% -> 0%
where the time goes in v1:
time: 103 us; the launch traced here: 101 us
  Pallas kernels  88.4 us (86%)
  local copies, waits for them, and re-layouts  12.8 us (12%)
    pallas_call x1, Pallas kernels, modes_call(): pl.pallas_call(modes_kernel, out_shape=jax.ShapeDtypeStruct((2, 4, 16, 16...  20.6 us
    pallas_call x1, Pallas kernels, weights_call(): pl.pallas_call(weights_kernel, out_shape=jax.ShapeDtypeStruct((8, 128), F...  16.7 us
    pallas_call x1, Pallas kernels, bands_call(): pl.pallas_call(bands_kernel, out_shape=jax.ShapeDtypeStruct((4, 16, 32, 1...  16.3 us
    pallas_call x1, Pallas kernels, spectra_call(): pl.pallas_call(spectra_kernel, out_shape=(jax.ShapeDtypeStruct((8, 128, 2...  15.8 us
    unnamed x20, local copies, waits for them, and re-layouts  11.3 us
    pallas_call x1, Pallas kernels, fourier_call(): pl.pallas_call(fourier_kernel, out_shape=jax.ShapeDtypeStruct((4, 16, 16,...  8.91 us
    pallas_call x1, Pallas kernels, layout_call(): pl.pallas_call(layout_kernel, out_shape=jax.ShapeDtypeStruct((64, 32, 128...  6.95 us
    pallas_call x1, Pallas kernels, clean_call(): pl.pallas_call(clean_kernel, out_shape=jax.ShapeDtypeStruct((4, 16, 32, 1...  3.22 us

profile of v1, /device:TPU:1, one launch (start us, length us, event | category | flops | bytes accessed | tf_op | source)
XLA Modules:
  0.0 101.4 jit_solution(17400220985043348361)
XLA Ops:
  0.0 0.0 copy-start.8
  0.0 0.0 copy-start.9
  0.0 0.7 broadcast_in_dim.12.widths_ref
  0.7 0.7 broadcast_in_dim.13
  1.4 0.1 reshape.20.m_ref
  1.5 0.0 copy-start
  1.5 3.4 %copy-done = bf16[1,16,32,8192]{3,2,1,0:T(8,128)(2,1)S(1)} copy-done((bf16[1,16,32,8192]{3,2,1,0:T(8,128)(2,1)S(1)}, bf16[1,16,32,8192]{3,2,1,0:T(8,128)(2,1)}, u32[]{:S(2)}) %copy-start) | copy-done | bytes 8388632
  4.9 8.9 %fourier.1.sb_ref = bf16[4,16,16,128]{3,2,1,0:T(8,128)(2,1)S(1)} custom-call(s32[1,256]{1,0:T(1,128)S(1)} %reshape.20.m_ref, bf16[512,8192]{1,0:T(8,128)(2,1)S(1)} %bitcast.6), custom_call_target="tpu_custom_call" | custom-call | tf_op jit(solution)/shard_map/fourier/pallas_call | solution.py:109
  13.8 0.0 copy-start.5
  13.9 0.7 copy-done.5
  14.6 20.6 %modes_exchange.1 = bf16[2,4,16,16,128]{4,3,2,1,0:T(8,128)(2,1)} custom-call(bf16[4,16,16,128]{3,2,1,0:T(8,128)(2,1)} %copy-done.5), custom_call_target="tpu_custom_call" | custom-call | tf_op jit(solution)/shard_map/modes_exchange/pallas_call | solution.py:253
  35.1 0.0 copy-done.8
  35.2 0.0 copy-done.9
  35.2 0.0 copy-start.3
  35.2 1.0 %copy-done.3 = bf16[2,4,16,16,128]{4,3,2,1,0:T(8,128)(2,1)S(1)} copy-done((bf16[2,4,16,16,128]{4,3,2,1,0:T(8,128)(2,1)S(1)}, bf16[2,4,16,16,128]{4,3,2,1,0:T(8,128)(2,1)}, u32[]{:S(2)}) %copy-start.3) | copy-done | bytes 524312
  36.2 15.8 %spectra.1 = (bf16[8,128,2048]{2,1,0:T(8,128)(2,1)S(1)}, f32[40,128]{1,0:T(8,128)S(1)}, bf16[2048,128]{1,0:T(8,128)(2,1)S(1)}) custom-call(s32[128]{0:T(128)S(1)} %copy-done.8, s32[1,256]{1,0:T(1,128)S(1)} %bitcast.8, s32[8,128]{1,0:T(8,128)S(1)} %broadcast_in_dim.12.widths_ref, bf16[2,4,256,128]{3,2,1,0:T(8,128)(2,1)S(1)} %bitcast.7, ...), custom_call_target="tpu_custom_call" | custom-call | tf_op jit(solution)/shard_map/spectra/pallas_call | solution.py:485
  52.0 0.0 copy-start.1
  52.0 1.9 %copy-done.1 = bf16[8,128,2048]{2,1,0:T(8,128)(2,1)} copy-done((bf16[8,128,2048]{2,1,0:T(8,128)(2,1)}, bf16[8,128,2048]{2,1,0:T(8,128)(2,1)S(1)}, u32[]{:S(2)}) %copy-start.1) | copy-done | bytes 4194328
  54.0 0.0 copy-start.6
  54.0 0.6 copy-done.6
  54.6 16.7 %weights.1.w_ref = f32[8,128]{1,0:T(8,128)} custom-call(f32[40,128]{1,0:T(8,128)} %copy-done.6), custom_call_target="tpu_custom_call" | custom-call | tf_op jit(solution)/shard_map/weights/pallas_call | solution.py:343
  71.3 0.0 copy-start.2
  71.3 2.2 %copy-done.2 = bf16[8,128,2048]{2,1,0:T(8,128)(2,1)S(1)} copy-done((bf16[8,128,2048]{2,1,0:T(8,128)(2,1)S(1)}, bf16[8,128,2048]{2,1,0:T(8,128)(2,1)}, u32[]{:S(2)}) %copy-start.2) | copy-done | bytes 4194328
  73.5 0.0 copy-start.7
  73.5 0.7 copy-done.7
  74.1 3.2 %weighted_sums.1.sb_ref = bf16[4,16,32,128]{3,2,1,0:T(8,128)(2,1)S(1)} custom-call(f32[8,128]{1,0:T(8,128)S(1)} %copy-done.7, bf16[2048,128]{1,0:T(8,128)(2,1)S(1)} %get-tuple-element.9.onehot_ref, bf16[8,128,2048]{2,1,0:T(8,128)(2,1)S(1)} %copy-done.2), custom_call_target="tpu_custom_call" | custom-call | tf_op jit(solution)/shard_map/weighted_sums/pallas_call | solution.py:537
  77.4 0.0 copy-start.4
  77.4 0.8 copy-done.4
  78.2 16.3 %bands_exchange.1.rb_ref = bf16[4,16,32,128]{3,2,1,0:T(8,128)(2,1)} custom-call(bf16[4,16,32,128]{3,2,1,0:T(8,128)(2,1)} %copy-done.4), custom_call_target="tpu_custom_call" | custom-call | tf_op jit(solution)/shard_map/bands_exchange/pallas_call | solution.py:376
  94.4 6.9 %output_layout.1 = f32[64,32,128]{2,1,0:T(8,128)} custom-call(bf16[4,16,32,128]{3,2,1,0:T(8,128)(2,1)} %bands_exchange.1.rb_ref), custom_call_target="tpu_custom_call" | custom-call | tf_op jit(solution)/shard_map/output_layout/pallas_call | solution.py:560
  (1 shorter events, 0.0 us)
Async XLA Ops:
  0.0 35.1 %copy-start.8 = (s32[128]{0:T(128)S(1)}, s32[128]{0:T(128)}, u32[]{:S(2)}) copy-start(s32[128]{0:T(128)} %mv_ref.1) | copy-start | bytes 1540
  0.0 35.2 %copy-start.9 = (s32[256]{0:T(256)S(1)}, s32[256]{0:T(256)}, u32[]{:S(2)}) copy-start(s32[256]{0:T(256)} %param.8) | copy-start | bytes 3076
  1.5 3.4 %copy-start = (bf16[1,16,32,8192]{3,2,1,0:T(8,128)(2,1)S(1)}, bf16[1,16,32,8192]{3,2,1,0:T(8,128)(2,1)}, u32[]{:S(2)}) copy-start(bf16[1,16,32,8192]{3,2,1,0:T(8,128)(2,1)} %param.5) | copy-start | bytes 25165828
  13.8 0.7 copy-start.5
  35.2 1.0 %copy-start.3 = (bf16[2,4,16,16,128]{4,3,2,1,0:T(8,128)(2,1)S(1)}, bf16[2,4,16,16,128]{4,3,2,1,0:T(8,128)(2,1)}, u32[]{:S(2)}) copy-start(bf16[2,4,16,16,128]{4,3,2,1,0:T(8,128)(2,1)} %modes_exchange.1) | copy-start | bytes 1572868
  52.0 1.9 %copy-start.1 = (bf16[8,128,2048]{2,1,0:T(8,128)(2,1)}, bf16[8,128,2048]{2,1,0:T(8,128)(2,1)S(1)}, u32[]{:S(2)}) copy-start(bf16[8,128,2048]{2,1,0:T(8,128)(2,1)S(1)} %get-tuple-element.10.coef_ref) | copy-start | bytes 12582916
  54.0 0.6 copy-start.6
  71.3 2.2 %copy-start.2 = (bf16[8,128,2048]{2,1,0:T(8,128)(2,1)S(1)}, bf16[8,128,2048]{2,1,0:T(8,128)(2,1)}, u32[]{:S(2)}) copy-start(bf16[8,128,2048]{2,1,0:T(8,128)(2,1)} %copy-done.1) | copy-start | bytes 12582916
  73.5 0.7 copy-start.7
  77.4 0.8 copy-start.4

commit v2 on v1

v2 whole, which is shorter than its diff:
```python
import functools
import math

import jax
import jax.numpy as jnp
from jax import lax
from jax.experimental import pallas as pl
from jax.experimental.pallas import tpu as pltpu
from jax.sharding import PartitionSpec as P

F32 = jnp.float32
BF16 = jnp.bfloat16
PIX = 8192
PAIRS = [(i, j) for i in range(8) for j in range(i, 8)]
PROWS = 40
MESH = pl.DeviceIdType.MESH
VMEM = pltpu.VMEM
DMA = pltpu.SemaphoreType.DMA


def vspec():
    return pl.BlockSpec(memory_space=pltpu.VMEM)


def split_dot(a, b, dims):
    hi = a.astype(BF16)
    rest = a - hi.astype(F32)
    mid = rest.astype(BF16)
    low = (rest - mid.astype(F32)).astype(BF16)
    out = lax.dot_general(low, b, dims, preferred_element_type=F32)
    out += lax.dot_general(mid, b, dims, preferred_element_type=F32)
    return out + lax.dot_general(hi, b, dims, preferred_element_type=F32)


NN = (((1,), (0,)), ((), ()))
NT = (((1,), (1,)), ((), ()))


def swap_blocks(arrays, width):
    count = len(arrays)
    block = lax.broadcasted_iota(jnp.int32, arrays[0].shape, 1) // width
    arrays = list(arrays)
    step = 1
    while step < count:
        low = (block // step) % 2 == 0
        for i in range(count):
            if i & step:
                continue
            a, b = arrays[i], arrays[i | step]
            arrays[i] = jnp.where(low, a, pltpu.roll(b, step * width, 1))
            arrays[i | step] = jnp.where(low, pltpu.roll(a, 128 - step * width, 1), b)
        step *= 2
    return arrays


CHUNKS = 16


def sky_copy(x_hbm, xbuf, sem, n):
    width = PIX // CHUNKS
    return pltpu.make_async_copy(
        x_hbm.at[:, pl.ds(pl.multiple_of(n * width, width), width)], xbuf.at[n], sem.at[n]
    )


def fourier_part(m_ref, x_hbm, sb_ref, xbuf, tab_a, tab_b, rows, sem):
    lax.fori_loop(0, CHUNKS, lambda n, _: (sky_copy(x_hbm, xbuf, sem, n).start(), 0)[1], 0)
    m = m_ref[...]
    step = jnp.float32(2.0 * math.pi / PIX)
    high = lax.broadcasted_iota(jnp.int32, (64, 256), 0)
    quarter = (lax.broadcasted_iota(jnp.int32, (64, 256), 1) // 8) % 2 * (PIX // 4)
    ang = (((high * m) % 64 * 128 + quarter) % PIX).astype(F32) * step
    factor = jnp.float32(PIX ** (-0.5))
    tab_a[0] = jnp.cos(ang) * factor
    tab_a[1] = jnp.sin(ang) * factor
    low = lax.broadcasted_iota(jnp.int32, (128, 256), 0)
    ang = ((low * m) % PIX).astype(F32) * step
    tab_b[0] = jnp.cos(ang)
    tab_b[1] = jnp.sin(ang)
    rows[...] = jnp.zeros_like(rows)

    def chunk(n, _):
        parts = []
        for u in range(4):
            ca = tab_a[0, pl.ds(n * 4 + u, 1), :]
            sa = tab_a[1, pl.ds(n * 4 + u, 1), :]
            parts.append((tab_b[0] * ca - tab_b[1] * sa).astype(BF16))
        table = jnp.concatenate(parts, axis=0)
        sky_copy(x_hbm, xbuf, sem, n).wait()
        out = jnp.dot(xbuf[n], table, preferred_element_type=F32)
        rows[0] += out[:, :128]
        rows[1] += out[:, 128:]
        return 0

    lax.fori_loop(0, CHUNKS, chunk, 0)

    for xg in range(4):
        for half in range(2):
            parts = [rows[half, pl.ds(xg * 8 + k, 16, stride=32), :] for k in range(8)]
            for g, part in enumerate(swap_blocks(parts, 16)):
                sb_ref[xg, half * 8 + g] = part.astype(BF16)


def place():
    freq = lax.axis_index("freq")
    blk = lax.axis_index("blk")
    return freq // 2, freq % 2, blk


def plane_peer(x, c, b, d):
    q = (x * 16 + b + d) % 64
    return (q // 16 * 2 + c, q % 16)


def plane_copy(src, dst, send, recv, x, c, b, d):
    q = (x * 16 + b + d) % 64
    return pltpu.make_async_remote_copy(
        src_ref=src.at[q // 16, q % 16],
        dst_ref=dst.at[x, b],
        send_sem=send.at[d],
        recv_sem=recv.at[x * 16 + b],
        device_id=(q // 16 * 2 + c, q % 16),
        device_id_type=MESH,
    )


def plane_arrival(src, dst, send, recv, x, c, b, p):
    return pltpu.make_async_remote_copy(
        src_ref=src.at[p // 16, p % 16],
        dst_ref=dst.at[p // 16, p % 16],
        send_sem=send.at[0],
        recv_sem=recv.at[p],
        device_id=(x * 2 + c, b),
        device_id_type=MESH,
    )


def plane_start(src, dst, send, recv, own, x, c, b):
    pltpu.make_async_copy(src.at[x, b], dst.at[x, b], own).start()

    def one(d, _):
        plane_copy(src, dst, send, recv, x, c, b, d).start()
        return 0

    lax.fori_loop(1, 64, one, 0)


def plane_send_wait(src, dst, send, recv, x, c, b):
    def one(d, _):
        plane_copy(src, dst, send, recv, x, c, b, d).wait_send()
        return 0

    lax.fori_loop(1, 64, one, 0)


def forward_copy(rb, fsend, frecv, x, c, b, core, g):
    return pltpu.make_async_remote_copy(
        src_ref=rb.at[core, g],
        dst_ref=rb.at[core, g],
        send_sem=fsend.at[g],
        recv_sem=frecv.at[g],
        device_id=(x * 2 + 1 - c, b),
        device_id_type=MESH,
    )


def wait_group(src, dst, send, recv, x, c, b, g):
    def one(j, _):
        p = g * 16 + j

        @pl.when(p != x * 16 + b)
        def _():
            plane_arrival(src, dst, send, recv, x, c, b, p).wait_recv()

        return 0

    lax.fori_loop(0, 16, one, 0)


def sum_over_devices(part, got, send, recv):
    x, c, b = place()
    y, z = b // 4, b % 4
    stages = [
        (3, lambda d: (x * 2 + c, y * 4 + (z + d) % 4)),
        (3, lambda d: (x * 2 + c, (y + d) % 4 * 4 + z)),
        (3, lambda d: ((x + d) % 4 * 2 + c, b)),
        (1, lambda d: (x * 2 + 1 - c, b)),
    ]
    base = 0
    for index, (count, peer) in enumerate(stages):
        copies = []
        for d in range(1, count + 1):
            copies.append(
                pltpu.make_async_remote_copy(
                    src_ref=part.at[index],
                    dst_ref=got.at[base + d - 1],
                    send_sem=send.at[base + d - 1],
                    recv_sem=recv.at[base + d - 1],
                    device_id=peer(d),
                    device_id_type=MESH,
                )
            )
        for copy in copies:
            copy.start()
        total = part[index]
        for d, copy in enumerate(copies):
            copy.wait_recv()
            total = total + got[base + d]
        part[index + 1] = total
        for copy in copies:
            copy.wait_send()
        base += count


def solve_bins(packed, matrix):
    for row, (i, j) in enumerate(PAIRS):
        value = packed[pl.ds(row, 1), :]
        matrix[j, pl.ds(i, 1), :] = value
        if i != j:
            matrix[i, pl.ds(j, 1), :] = value
    columns = [matrix[j] for j in range(8)]
    rows = lax.broadcasted_iota(jnp.int32, (8, 128), 0)
    trace = sum(columns[j][j : j + 1] for j in range(8))
    load = jnp.float32(0.1) * trace / jnp.float32(8)
    columns = [columns[j] + jnp.where(rows == j, load, 0.0) for j in range(8)]
    z = jnp.ones((8, 128), F32)
    for j in range(8):
        pivot = columns[j][j : j + 1]
        scale = columns[j] / pivot
        keep = rows == j
        for k in range(j + 1, 8):
            columns[k] = columns[k] - jnp.where(keep, 0.0, scale * columns[k][j : j + 1])
        z = z - jnp.where(keep, 0.0, scale * z[j : j + 1])
        columns[j] = jnp.where(keep, columns[j], 0.0)
    diagonal = sum(columns)
    z = z / diagonal
    return z / jnp.sum(z, axis=0, keepdims=True)


def legendre_copy(leg_hbm, leg, sem, c, i):
    start = pl.multiple_of((i % 4 * 2 + c) * 512, 512)
    return pltpu.make_async_copy(
        leg_hbm.at[i // 4, :, pl.ds(start, 512)], leg.at[i // 4, i % 4], sem.at[i]
    )


def bin_rows(widths_ref, c, onehot):
    row = lax.broadcasted_iota(jnp.int32, (128, 128), 0)
    col = lax.broadcasted_iota(jnp.int32, (128, 128), 1)
    upper = jnp.where(row <= col, 1.0, 0.0).astype(BF16)
    widths = widths_ref[...].astype(F32)
    ends = split_dot(widths, upper, NN)
    begins = ends - widths
    ends, begins = ends[0:1], begins[0:1]

    def chunk(g, _):
        ell = lax.broadcasted_iota(jnp.int32, (512, 128), 0) + ((g * 2 + c) * 512)
        ell = ell.astype(F32)
        hit = jnp.where(ell >= begins, 1.0, 0.0) * jnp.where(ell < ends, 1.0, 0.0)
        onehot[pl.ds(pl.multiple_of(g * 512, 512), 512), :] = hit.astype(BF16)
        return 0

    lax.fori_loop(0, 4, chunk, 0)


def order_channel(rb, perm, left, turned, core, g):
    ch = g * 2 + core
    block = rb[core, g].reshape(256, 128)
    sorted_rows = jnp.dot(perm[...], block, preferred_element_type=F32)
    for h in range(2):
        turned[h] = sorted_rows[h * 128 : h * 128 + 128].T
        for s in range(8):
            left[s, pl.ds(pl.multiple_of(ch * 16, 16), 16), h * 128 : h * 128 + 128] = turned[
                h, pl.ds(s, 16, stride=8), :
            ].astype(BF16)


def legendre_sums(leg_hbm, leg, sem, c, left, coef):
    def one(i, _):
        legendre_copy(leg_hbm, leg, sem, c, i).wait()
        out = jnp.dot(left[i // 4], leg[i // 4, i % 4], preferred_element_type=F32)
        coef[i // 4, :, pl.ds(pl.multiple_of(i % 4 * 512, 512), 512)] = out.astype(BF16)
        return 0

    lax.fori_loop(0, 32, one, 0)


def cross_spectra(coef, mult, sums, per_ell):
    def tile(t, _):
        lanes = pl.ds(pl.multiple_of(t * 128, 128), 128)
        acc = [jnp.zeros((8, 128), F32) for _ in PAIRS]

        def slot(s, acc):
            acc = list(acc)
            for half in range(1):
                values = [coef[s, i * 16 : i * 16 + 16, lanes].astype(F32) for i in range(8)]
                factor = mult(s)
                scaled = [v * factor for v in values]
                for n, (i, j) in enumerate(PAIRS):
                    prod = scaled[i] * values[j]
                    acc[n] = acc[n] + (prod[0:8] + prod[8:16])
            return tuple(acc)

        acc = lax.fori_loop(0, 8, slot, tuple(acc))
        for n, value in enumerate(acc):
            sums[n * 8 : n * 8 + 8, :] = value
        total = sums[pl.ds(0, PROWS, stride=8), :]
        for r in range(1, 8):
            total = total + sums[pl.ds(r, PROWS, stride=8), :]
        per_ell[:, lanes] = total
        return 0

    sums[...] = jnp.zeros_like(sums)
    lax.fori_loop(0, 16, tile, 0)


def slot_mult(mv_ref, b):
    return lambda s: (1 + jnp.minimum(mv_ref[b * 8 + s], 1)).astype(F32)


def weighted_sums(coef, weights, onehot, table, turned, sb):
    table[...] = split_dot(weights, onehot[...], NT)

    def tile(t, _):
        lanes = pl.ds(pl.multiple_of(t * 128, 128), 128)
        per = [jnp.broadcast_to(table[i : i + 1, lanes], (16, 128)) for i in range(8)]
        for s in range(8):
            total = per[0] * coef[s, 0:16, lanes].astype(F32)
            for i in range(1, 8):
                total += per[i] * coef[s, i * 16 : i * 16 + 16, lanes].astype(F32)
            turned[pl.ds(s, 16, stride=8), :] = total
        parts = [turned[i * 32 : i * 32 + 32, :] for i in range(4)]
        for j, part in enumerate(swap_blocks(parts, 32)):
            sb[t // 4, t % 4 * 4 + j] = part.astype(BF16)
        return 0

    lax.fori_loop(0, 16, tile, 0)


def output_group(rb, out, x):
    for pair in range(2):
        parts = [rb[x, b, pair * 16 : pair * 16 + 16, :].astype(F32) for b in range(16)]
        for k in range(2):
            block = jnp.concatenate([p[k * 8 : k * 8 + 8] for p in parts], axis=0).T
            for i in range(4):
                out[x * 16 + i * 4 + pair * 2 + k] = block[i * 32 : i * 32 + 32]


def kernel(
    mv_ref, m_ref, order_ref, widths_ref, sky_hbm, leg_hbm, out_ref,
    xbuf, tab_a, tab_b, rows, sb1, rb1, perm, left, turned2, leg, coef, sums, per_ell,
    onehot, part, got, matrix, table, turned, sb3, rb3,
    sky_sem, leg_sem, send1, recv1, fsend, frecv, send2, recv2, send3, recv3, own,
):
    x, c, b = place()
    barrier = pltpu.get_barrier_semaphore()

    def hello(d, _):
        pl.semaphore_signal(barrier, device_id=plane_peer(x, c, b, d), device_id_type=MESH)
        return 0

    lax.fori_loop(1, 64, hello, 0)
    pl.semaphore_signal(barrier, device_id=(x * 2 + 1 - c, b), device_id_type=MESH)
    fourier_part(m_ref, sky_hbm, sb1, xbuf, tab_a, tab_b, rows, sky_sem)
    lax.fori_loop(0, 32, lambda i, _: (legendre_copy(leg_hbm, leg, leg_sem, c, i).start(), 0)[1], 0)

    pl.semaphore_wait(barrier, 64)
    mine = rb1.at[c]
    plane_start(sb1, mine, send1, recv1, own, x, c, b)
    bin_rows(widths_ref, c, onehot)
    q = lax.broadcasted_iota(jnp.int32, (256, 256), 0)
    perm[...] = jnp.where(q == order_ref[...], 1.0, 0.0).astype(BF16)
    pltpu.make_async_copy(sb1.at[x, b], mine.at[x, b], own).wait()

    def from_chips(i, _):
        g = (x + i) % 4
        wait_group(sb1, mine, send1, recv1, x, c, b, g)
        forward_copy(rb1, fsend, frecv, x, c, b, c, g).start()
        order_channel(rb1, perm, left, turned2, c, g)
        return 0

    lax.fori_loop(0, 4, from_chips, 0)

    def from_core(i, _):
        g = (x + i) % 4
        forward_copy(rb1, fsend, frecv, x, c, b, 1 - c, g).wait_recv()
        order_channel(rb1, perm, left, turned2, 1 - c, g)
        return 0

    lax.fori_loop(0, 4, from_core, 0)
    legendre_sums(leg_hbm, leg, leg_sem, c, left, coef)
    cross_spectra(coef, slot_mult(mv_ref, b), sums, per_ell)
    part[0] = split_dot(per_ell[...], onehot[...], NN)
    sum_over_devices(part, got, send2, recv2)
    weights = solve_bins(part.at[4], matrix)
    weighted_sums(coef, weights, onehot, table, turned, sb3)

    plane_start(sb3, rb3, send3, recv3, own, x, c, b)
    pltpu.make_async_copy(sb3.at[x, b], rb3.at[x, b], own).wait()

    def finish(i, _):
        g = (x + i) % 4
        wait_group(sb3, rb3, send3, recv3, x, c, b, g)
        output_group(rb3, out_ref, g)
        return 0

    lax.fori_loop(0, 4, finish, 0)
    plane_send_wait(sb1, mine, send1, recv1, x, c, b)
    lax.fori_loop(
        0, 4, lambda g, _: (forward_copy(rb1, fsend, frecv, x, c, b, c, g).wait_send(), 0)[1], 0
    )
    plane_send_wait(sb3, rb3, send3, recv3, x, c, b)


def on_device(sky_maps, legendre, mode_values, cycle_order, bin_widths):
    sky = sky_maps.reshape(512, PIX)
    slots = mode_values.reshape(16, 1, 8)
    mcol = jnp.broadcast_to(slots, (16, 2, 8)).reshape(1, 256)
    order = cycle_order.reshape(1, 256)
    widths = jnp.broadcast_to(bin_widths.reshape(1, 128), (8, 128))
    hbm = pl.BlockSpec(memory_space=pltpu.HBM)
    out = pl.pallas_call(
        kernel,
        out_shape=jax.ShapeDtypeStruct((64, 32, 128), F32),
        in_specs=[pl.BlockSpec(memory_space=pltpu.SMEM), vspec(), vspec(), vspec(), hbm, hbm],
        out_specs=vspec(),
        scratch_shapes=[
            VMEM((CHUNKS, 512, PIX // CHUNKS), BF16),
            VMEM((2, 64, 256), F32),
            VMEM((2, 128, 256), F32),
            VMEM((2, 512, 128), F32),
            VMEM((4, 16, 16, 128), BF16),
            VMEM((2, 4, 16, 16, 128), BF16),
            VMEM((256, 256), BF16),
            VMEM((8, 128, 256), BF16),
            VMEM((2, 128, 128), F32),
            VMEM((8, 4, 256, 512), BF16),
            VMEM((8, 128, 2048), BF16),
            VMEM((PROWS * 8, 128), F32),
            VMEM((PROWS, 2048), F32),
            VMEM((2048, 128), BF16),
            VMEM((5, PROWS, 128), F32),
            VMEM((10, PROWS, 128), F32),
            VMEM((8, 8, 128), F32),
            VMEM((8, 2048), F32),
            VMEM((128, 128), F32),
            VMEM((4, 16, 32, 128), BF16),
            VMEM((4, 16, 32, 128), BF16),
            DMA((CHUNKS,)),
            DMA((32,)),
            DMA((64,)),
            DMA((64,)),
            DMA((4,)),
            DMA((4,)),
            DMA((10,)),
            DMA((10,)),
            DMA((64,)),
            DMA((64,)),
            DMA,
        ],
        compiler_params=pltpu.CompilerParams(
            collective_id=0, has_side_effects=True, vmem_limit_bytes=48 << 20
        ),
        name="harmonic_ilc",
    )(mode_values, mcol, order, widths, sky, legendre)
    return out.reshape(32, 2, 32, 128).transpose(0, 1, 3, 2)


def solution(mesh):
    return jax.shard_map(
        on_device,
        mesh=mesh,
        in_specs=(P("freq", "blk", None, None), P("blk", None, None), P(), P(), P()),
        out_specs=P(None, None, None, ("freq", "blk")),
        check_vma=False,
    )
```

time: 103 us -> 72.1 us (0.70); the launches traced: 101 us -> 72 us
  Pallas kernels: 88.4 us -> 68.2 us
  local copies, waits for them, and re-layouts: 12.8 us -> 3.8 us
    pallas_call x7 -> x1, Pallas kernels: 88.4 us -> 68.2 us  [on_device(): pl.pallas_call(kernel, out_shape=jax.ShapeDtypeStruct((64, 32, 128), F32)...]
    unnamed x20 -> x5, local copies, waits for them, and re-layouts: 11.3 us -> 2.3 us
where the time goes in v2:
time: 72.1 us; the launch traced here: 72 us
  Pallas kernels  68.2 us (95%)
  local copies, waits for them, and re-layouts  3.8 us (5%)
    pallas_call x1, Pallas kernels, on_device(): pl.pallas_call(kernel, out_shape=jax.ShapeDtypeStruct((64, 32, 128), F32)...  68.2 us
    unnamed x5, local copies, waits for them, and re-layouts  2.3 us

profile of v2, /device:TPU:1, one launch (start us, length us, event | category | flops | bytes accessed | tf_op | source)
XLA Modules:
  0.0 72.0 jit_solution(1209336767842205114)
XLA Ops:
  0.0 0.7 broadcast_in_dim.14.widths_ref
  0.7 0.7 %broadcast_in_dim.12 = s32[16,8]{1,0:T(8,128)S(1)} reshape(s32[128]{0:T(128)} %mv_ref.1) | data formatting | bytes 1024 | tf_op jit(solution)/shard_map/broadcast_in_dim | solution.py:418
  1.4 0.1 reshape.16.m_ref
  1.5 0.0 copy-start
  1.5 0.6 copy-done
  2.2 0.0 copy-start.1
  2.2 0.7 copy-done.1
  2.8 68.2 %harmonic_ilc.1 = f32[64,32,128]{2,1,0:T(8,128)S(1)} custom-call(s32[128]{0:T(128)S(1)} %copy-done, s32[1,256]{1,0:T(1,128)S(1)} %reshape.16.m_ref, s32[1,256]{1,0:T(1,128)S(1)} %bitcast.6, s32[8,128]{1,0:T(8,128)S(1)} %broadcast_in_dim.14.widths_ref, bf16[512,8192]{1,0:T(8,128)(2,1)} %bitcast.7, bf16[8,256,4096]{2,1,0:T(8,128)(2,1)} %leg_hbm.1), custom_call_target="tpu_custom_call" | custom-call | tf_op jit(solution)/shard_map/harmonic_ilc/pallas_call | solution.py:422
  71.0 1.0 %copy.7 = f32[32,2,128,32]{2,3,1,0:T(8,128)} copy(f32[32,2,128,32]{2,3,1,0:T(8,128)S(1)} %bitcast.5) | data formatting | bytes 2097152
  (1 shorter events, 0.0 us)
Async XLA Ops:
  1.5 0.7 copy-start
  2.2 0.7 copy-start.1

commit v3 on v0

v3 whole, which is shorter than its diff:
```python
import math

import jax
import jax.numpy as jnp
from jax import lax
from jax.experimental import pallas as pl
from jax.experimental.pallas import tpu as pltpu
from jax.sharding import PartitionSpec as P

F32 = jnp.float32
BF16 = jnp.bfloat16
PIX = 8192
CHUNKS = 16
WIDTH = PIX // CHUNKS
PAIRS = [(i, j) for i in range(8) for j in range(i, 8)]
PROWS = 40
PARTS = [(0, 16), (16, 16), (32, 8)]
MESH = pl.DeviceIdType.MESH
VMEM = pltpu.VMEM
DMA = pltpu.SemaphoreType.DMA
NN = (((1,), (0,)), ((), ()))
NT = (((1,), (1,)), ((), ()))


def hops(d):
    return min(d, 4 - d)


OFFSETS = sorted(((dy, dz) for dy in range(4) for dz in range(4)), key=lambda t: -hops(t[0]) - hops(t[1]))


def split_dot(a, b, dims):
    hi = a.astype(BF16)
    rest = a - hi.astype(F32)
    mid = rest.astype(BF16)
    low = (rest - mid.astype(F32)).astype(BF16)
    out = lax.dot_general(low, b, dims, preferred_element_type=F32)
    out += lax.dot_general(mid, b, dims, preferred_element_type=F32)
    return out + lax.dot_general(hi, b, dims, preferred_element_type=F32)


def swap_blocks(arrays, width):
    count = len(arrays)
    block = lax.broadcasted_iota(jnp.int32, arrays[0].shape, 1) // width
    arrays = list(arrays)
    step = 1
    while step < count:
        low = (block // step) % 2 == 0
        for i in range(count):
            if i & step:
                continue
            a, b = arrays[i], arrays[i | step]
            arrays[i] = jnp.where(low, a, pltpu.roll(b, step * width, 1))
            arrays[i | step] = jnp.where(low, pltpu.roll(a, 128 - step * width, 1), b)
        step *= 2
    return arrays


def turn(phase):
    quadrant = (phase + PIX // 8) // (PIX // 4)
    a = (phase - quadrant * (PIX // 4)).astype(F32) * jnp.float32(2.0 * math.pi / PIX)
    a2 = a * a
    s = jnp.float32(1 / 362880)
    for coefficient in (-1 / 5040, 1 / 120, -1 / 6, 1.0):
        s = s * a2 + jnp.float32(coefficient)
    s = s * a
    c = jnp.float32(-1 / 3628800)
    for coefficient in (1 / 40320, -1 / 720, 1 / 24, -1 / 2, 1.0):
        c = c * a2 + jnp.float32(coefficient)
    odd = quadrant % 2 == 1
    cosine = jnp.where(odd, s, c)
    sine = jnp.where(odd, c, s)
    cosine = jnp.where((quadrant + 1) % 4 >= 2, -cosine, cosine)
    sine = jnp.where(quadrant % 4 >= 2, -sine, sine)
    return cosine, sine


def wrap(v):
    return lax.rem(v, 4)


class Place:
    def __init__(self):
        freq = lax.axis_index("freq")
        self.b = lax.axis_index("blk")
        self.x, self.c = lax.div(freq, 2), lax.rem(freq, 2)
        self.y, self.z = lax.div(self.b, 4), lax.rem(self.b, 4)
        self.p = self.x * 16 + self.b
        self.partner = (self.x * 2 + 1 - self.c, self.b)

    def device(self, x, y, z):
        return (x * 2 + self.c, y * 4 + z)


def remote(src, dst, send, recv, device):
    return pltpu.make_async_remote_copy(
        src_ref=src, dst_ref=dst, send_sem=send, recv_sem=recv, device_id=device, device_id_type=MESH
    )


def wait_blocks(blocks, sem, count):
    part = blocks.at[pl.ds(0, count)]
    pltpu.make_async_copy(part, part, sem).wait()


def sky_copy(sky_hbm, xbuf, sem, n):
    return pltpu.make_async_copy(
        sky_hbm.at[:, pl.ds(pl.multiple_of(n * WIDTH, WIDTH), WIDTH)], xbuf.at[n], sem.at[n]
    )


def make_tables(modes, tab_a, tab_b):
    m = modes[...]
    factor = jnp.float32(PIX ** (-0.5))
    high = lax.broadcasted_iota(jnp.int32, (64, 128), 0)
    cosine, sine = turn((high * m) % 64 * 128)
    tab_a[0] = cosine * factor
    tab_a[1] = sine * factor
    low = lax.broadcasted_iota(jnp.int32, (128, 128), 0)
    cosine, sine = turn((low * m) % PIX)
    tab_b[0] = cosine
    tab_b[1] = sine


def make_chunk(tab_a, tab_b, table, n):
    for u in range(4):
        ca = tab_a[0, pl.ds(n * 4 + u, 1), :]
        sa = tab_a[1, pl.ds(n * 4 + u, 1), :]
        lines = slice(u * 128, u * 128 + 128)
        table[lines, 0:128] = (tab_b[0] * ca - tab_b[1] * sa).astype(BF16)
        table[lines, 128:256] = (tab_b[1] * (-ca) - tab_b[0] * sa).astype(BF16)


def fourier_rows(sky_hbm, xbuf, sem, tab_a, tab_b, table, rows):
    make_chunk(tab_a, tab_b, table.at[0], 0)
    rows[...] = jnp.zeros_like(rows)

    def chunk(n, _):
        sky_copy(sky_hbm, xbuf, sem, n).wait()
        now = lax.rem(n, 2)
        out = jnp.dot(xbuf[n], table[now], preferred_element_type=F32)
        make_chunk(tab_a, tab_b, table.at[1 - now], lax.rem(n + 1, CHUNKS))
        rows[0] += out[:, :128]
        rows[1] += out[:, 128:]
        return 0

    lax.fori_loop(0, CHUNKS, chunk, 0)


def legendre_copy(leg_hbm, leg, sem, c, u):
    start = (u // 2 * 2 + c) * 512 + u % 2 * 256
    return pltpu.make_async_copy(
        leg_hbm.at[:, :, pl.ds(pl.multiple_of(start, 256), 256)], leg.at[u], sem.at[u]
    )


def bin_columns(widths, c, onehot):
    row = lax.broadcasted_iota(jnp.int32, (128, 128), 0)
    col = lax.broadcasted_iota(jnp.int32, (128, 128), 1)
    upper = jnp.where(row <= col, 1.0, 0.0).astype(BF16)
    wide = jnp.broadcast_to(widths[...].astype(F32), (8, 128))
    ends = split_dot(wide, upper, NN)
    begins = ends - wide
    ends = jnp.broadcast_to(ends[0:1], (128, 128)).T
    begins = jnp.broadcast_to(begins[0:1], (128, 128)).T
    lane = lax.broadcasted_iota(jnp.int32, (128, 128), 1)

    def tile(t, _):
        ell = (lane + ((t // 4 * 2 + c) * 512 + t % 4 * 128)).astype(F32)
        hit = jnp.where(ell >= begins, 1.0, 0.0) * jnp.where(ell < ends, 1.0, 0.0)
        onehot[:, pl.ds(pl.multiple_of(t * 128, 128), 128)] = hit.astype(BF16)
        return 0

    lax.fori_loop(0, 16, tile, 0)


def mode_factors(modes, b, factors):
    lane = lax.broadcasted_iota(jnp.int32, (1, 128), 1)
    factor = (1 + jnp.minimum(modes[...], 1)).astype(F32)
    for s in range(8):
        one = jnp.sum(jnp.where(lane == b * 8 + s, factor, 0.0), axis=1, keepdims=True)
        factors[pl.ds(s, 1), :] = jnp.broadcast_to(one, (1, 128))


def order_channel(rb, perm, left, turned, core, g):
    ch = g * 2 + core
    block = rb[core, pl.ds(pl.multiple_of(g * 16, 16), 16)].reshape(256, 128)
    sorted_rows = jnp.dot(perm[...], block, preferred_element_type=F32)
    for h in range(2):
        turned[h] = sorted_rows[h * 128 : h * 128 + 128].T
    for h in range(2):
        for s in range(8):
            left[s, pl.ds(pl.multiple_of(ch * 16, 16), 16), h * 128 : h * 128 + 128] = turned[
                h, pl.ds(s, 16, stride=8), :
            ].astype(BF16)


def legendre_group(leg, left, coef, u):
    lanes = pl.ds(pl.multiple_of(u * 256, 256), 256)
    for s in range(8):
        out = jnp.dot(left[s], leg[u, s], preferred_element_type=F32)
        coef[s, :, lanes] = out.astype(BF16)


def spectra_group(coef, factors, sums, per_ell, onehot, total, u):
    for h in range(2):
        lanes = pl.ds(pl.multiple_of(u * 256 + h * 128, 128), 128)
        acc = [None] * len(PAIRS)
        for s in range(8):
            both = [coef[s, i * 16 : i * 16 + 16, lanes].astype(F32) for i in range(8)]
            factor = factors[pl.ds(s, 1), :]
            for half in range(2):
                values = [v[half * 8 : half * 8 + 8] for v in both]
                scaled = [v * factor for v in values]
                for n, (i, j) in enumerate(PAIRS):
                    product = scaled[i] * values[j]
                    acc[n] = product if acc[n] is None else acc[n] + product
        for n, value in enumerate(acc):
            sums[h, n * 8 : n * 8 + 8, :] = value
        line = sums[h, pl.ds(0, PROWS, stride=8), :]
        for r in range(1, 8):
            line = line + sums[h, pl.ds(r, PROWS, stride=8), :]
        per_ell[:, h * 128 : h * 128 + 128] = line
    group = pl.ds(pl.multiple_of(u * 256, 256), 256)
    total[...] += split_dot(per_ell[...], onehot[:, group], NT)


def legendre_spectra(leg_hbm, leg, sem, c, left, coef, factors, sums, per_ell, onehot, total):
    sums[...] = jnp.zeros_like(sums)
    total[...] = jnp.zeros_like(total)
    legendre_copy(leg_hbm, leg, sem, c, 0).wait()
    legendre_group(leg, left, coef, 0)

    def step(u, _):
        legendre_copy(leg_hbm, leg, sem, c, u + 1).wait()
        legendre_group(leg, left, coef, u + 1)
        spectra_group(coef, factors, sums, per_ell, onehot, total, u)
        return 0

    lax.fori_loop(0, 7, step, 0)
    spectra_group(coef, factors, sums, per_ell, onehot, total, 7)


def sum_over_devices(me, part, got, send, recv):
    x, y, z = me.x, me.y, me.z
    peers = [
        [me.device(x, y, wrap(z + d)) for d in (2, 1, 3)],
        [me.device(x, wrap(y + d), z) for d in (2, 1, 3)],
        [me.device(wrap(x + d), y, z) for d in (2, 1, 3)],
    ]
    started = []

    def go(stage, index):
        first, count = PARTS[index]
        lines = pl.ds(first, count)
        devices = peers[(stage + index) % 3] if stage < 3 else [me.partner]
        copies = []
        for d, device in enumerate(devices):
            n = (stage * 3 + index) * 3 + d
            copies.append(
                remote(
                    part.at[stage, lines], got.at[stage, d, lines], send.at[n], recv.at[n], device
                )
            )
            copies[-1].start()
        started.extend(copies)
        return copies

    flights = [go(0, index) for index in range(3)]
    for stage in range(4):
        later = []
        for index in range(3):
            first, count = PARTS[index]
            lines = pl.ds(first, count)
            value = part[stage, lines, :]
            for d, copy in enumerate(flights[index]):
                copy.wait_recv()
                value = value + got[stage, d, lines, :]
            part[stage + 1, lines, :] = value
            if stage < 3:
                later.append(go(stage + 1, index))
        flights = later
    return started


def solve_bins(packed, matrix):
    for row, (i, j) in enumerate(PAIRS):
        value = packed[pl.ds(row, 1), :]
        matrix[j, pl.ds(i, 1), :] = value
        if i != j:
            matrix[i, pl.ds(j, 1), :] = value
    columns = [matrix[j] for j in range(8)]
    rows = lax.broadcasted_iota(jnp.int32, (8, 128), 0)
    trace = sum(columns[j][j : j + 1] for j in range(8))
    load = jnp.float32(0.1) * trace / jnp.float32(8)
    columns = [columns[j] + jnp.where(rows == j, load, 0.0) for j in range(8)]
    z = jnp.ones((8, 128), F32)
    for j in range(8):
        pivot = columns[j][j : j + 1]
        scale = columns[j] / pivot
        keep = rows == j
        for k in range(j + 1, 8):
            columns[k] = columns[k] - jnp.where(keep, 0.0, scale * columns[k][j : j + 1])
        z = z - jnp.where(keep, 0.0, scale * z[j : j + 1])
        columns[j] = jnp.where(keep, columns[j], 0.0)
    z = z / sum(columns)
    return z / jnp.sum(z, axis=0, keepdims=True)


def weighted_tile(coef, table, turned, t):
    lanes = pl.ds(pl.multiple_of(t * 128, 128), 128)
    per = [jnp.broadcast_to(table[pl.ds(i, 1), lanes], (16, 128)) for i in range(8)]
    for s in range(8):
        total = per[0] * coef[s, 0:16, lanes].astype(F32)
        for i in range(1, 8):
            total += per[i] * coef[s, i * 16 : i * 16 + 16, lanes].astype(F32)
        turned[pl.ds(s, 16, stride=8), :] = total
    parts = [turned[i * 32 : i * 32 + 32, :] for i in range(4)]
    return swap_blocks(parts, 32)


def output_group(rb, out, x):
    for pair in range(2):
        parts = [rb[x * 16 + b, pair * 16 : pair * 16 + 16, :].astype(F32) for b in range(16)]
        for k in range(2):
            block = jnp.concatenate([p[k * 8 : k * 8 + 8] for p in parts], axis=0).T
            for i in range(4):
                out[x * 16 + i * 4 + pair * 2 + k] = block[i * 32 : i * 32 + 32]


def kernel(
    modes_hbm, order_hbm, widths_hbm, sky_hbm, leg_hbm, out_ref,
    modes, order, widths, xbuf, tab_a, tab_b, table, rows, sb1, rb1, perm, left, turned2, leg,
    coef, sums, per_ell, onehot, factors, part, got, matrix, spread, turned, sb3, rb3,
    small_sem, sky_sem, leg_sem, send1, recv1, fsend, frecv, send2, recv2, send3, recv3, own,
):
    me = Place()
    x, c, b = me.x, me.c, me.b
    small = [
        pltpu.make_async_copy(modes_hbm, modes, small_sem.at[0]),
        pltpu.make_async_copy(order_hbm, order, small_sem.at[1]),
        pltpu.make_async_copy(widths_hbm, widths, small_sem.at[2]),
    ]
    for copy in small:
        copy.start()
    for n in range(CHUNKS):
        sky_copy(sky_hbm, xbuf, sky_sem, n).start()
    for u in range(8):
        legendre_copy(leg_hbm, leg, leg_sem, c, u).start()
    barrier = pltpu.get_barrier_semaphore()
    for i in range(4):
        for dy, dz in OFFSETS:
            if i or dy or dz:
                device = me.device(wrap(x + i), wrap(me.y + dy), wrap(me.z + dz))
                pl.semaphore_signal(barrier, device_id=device, device_id_type=MESH)
    pl.semaphore_signal(barrier, device_id=me.partner, device_id_type=MESH)
    for copy in small:
        copy.wait()
    make_tables(modes, tab_a, tab_b)
    fourier_rows(sky_hbm, xbuf, sky_sem, tab_a, tab_b, table, rows)
    pl.semaphore_wait(barrier, 64)

    for i in (2, 1, 3, 0):
        xx = wrap(x + i)
        parts = [
            rows[half, pl.ds(xx * 8 + k, 16, stride=32), :] for k in range(8) for half in range(2)
        ]
        for g, block in enumerate(swap_blocks(parts, 8)):
            sb1[xx * 16 + g] = block.astype(BF16)
        for dy, dz in OFFSETS:
            if i or dy or dz:
                yy, zz = wrap(me.y + dy), wrap(me.z + dz)
                remote(
                    sb1.at[xx * 16 + yy * 4 + zz], rb1.at[c, me.p], send1, recv1.at[x],
                    me.device(xx, yy, zz),
                ).start()
    local = pltpu.make_async_copy(sb1.at[me.p], rb1.at[c, me.p], own)
    local.start()
    bin_columns(widths, c, onehot)
    mode_factors(modes, b, factors)
    q = lax.broadcasted_iota(jnp.int32, (256, 256), 0)
    perm[...] = jnp.where(q == order[...], 1.0, 0.0).astype(BF16)
    local.wait()

    def forward(core, g):
        lines = pl.ds(g * 16, 16)
        return remote(
            rb1.at[core, lines], rb1.at[core, lines], fsend.at[g], frecv.at[g], me.partner
        )

    for i in (2, 1, 3, 0):
        g = wrap(x + i)
        wait_blocks(rb1.at[c], recv1.at[g], 16 if i else 15)
        forward(c, g).start()
        order_channel(rb1, perm, left, turned2.at[0], c, g)
    for i in (2, 1, 3, 0):
        g = wrap(x + i)
        forward(1 - c, g).wait_recv()
        order_channel(rb1, perm, left, turned2.at[1], 1 - c, g)

    legendre_spectra(
        leg_hbm, leg, leg_sem, c, left, coef, factors, sums, per_ell, onehot, part.at[0]
    )
    started = sum_over_devices(me, part, got, send2, recv2)
    weights = solve_bins(part.at[4], matrix)
    spread[...] = split_dot(weights, onehot[...], NN)

    def tile(n, _):
        xx, yy = wrap(x + 1 + n // 4), wrap(me.y + 1 + n % 4)
        for zz, block in enumerate(
            weighted_tile(coef, spread, turned.at[lax.rem(n, 2)], xx * 4 + yy)
        ):
            sb3[xx * 16 + yy * 4 + zz] = block.astype(BF16)
        for zz in range(4):
            remote(
                sb3.at[xx * 16 + yy * 4 + zz], rb3.at[me.p], send3, recv3.at[x],
                me.device(xx, yy, zz),
            ).start()
        return 0

    lax.fori_loop(0, 15, tile, 0)
    for zz, block in enumerate(weighted_tile(coef, spread, turned.at[1], x * 4 + me.y)):
        sb3[x * 16 + me.y * 4 + zz] = block.astype(BF16)
    for d in (2, 1, 3):
        zz = wrap(me.z + d)
        remote(
            sb3.at[x * 16 + me.y * 4 + zz], rb3.at[me.p], send3, recv3.at[x],
            me.device(x, me.y, zz),
        ).start()
    local = pltpu.make_async_copy(sb3.at[me.p], rb3.at[me.p], own)
    local.start()
    for copy in started:
        copy.wait_send()
    for g in range(4):
        forward(c, g).wait_send()
    wait_blocks(sb1, send1, 63)
    local.wait()
    for i in (3, 2, 1, 0):
        g = wrap(x + i)
        wait_blocks(rb3, recv3.at[g], 16 if i else 15)
        output_group(rb3, out_ref, g)
    wait_blocks(sb3, send3, 63)


def on_device(sky_maps, legendre, mode_values, cycle_order, bin_widths):
    hbm = pl.BlockSpec(memory_space=pltpu.HBM)
    out = pl.pallas_call(
        kernel,
        out_shape=jax.ShapeDtypeStruct((64, 32, 128), F32),
        in_specs=[hbm] * 5,
        out_specs=pl.BlockSpec(memory_space=pltpu.VMEM),
        scratch_shapes=[
            VMEM((1, 128), jnp.int32),
            VMEM((1, 256), jnp.int32),
            VMEM((1, 128), jnp.int32),
            VMEM((CHUNKS, 512, WIDTH), BF16),
            VMEM((2, 64, 128), F32),
            VMEM((2, 128, 128), F32),
            VMEM((2, WIDTH, 256), BF16),
            VMEM((2, 512, 128), F32),
            VMEM((64, 16, 128), BF16),
            VMEM((2, 64, 16, 128), BF16),
            VMEM((256, 256), BF16),
            VMEM((8, 128, 256), BF16),
            VMEM((2, 2, 128, 128), F32),
            VMEM((8, 8, 256, 256), BF16),
            VMEM((8, 128, 2048), BF16),
            VMEM((2, PROWS * 8, 128), F32),
            VMEM((PROWS, 256), F32),
            VMEM((128, 2048), BF16),
            VMEM((8, 128), F32),
            VMEM((5, PROWS, 128), F32),
            VMEM((4, 3, PROWS, 128), F32),
            VMEM((8, 8, 128), F32),
            VMEM((8, 2048), F32),
            VMEM((2, 128, 128), F32),
            VMEM((64, 32, 128), BF16),
            VMEM((64, 32, 128), BF16),
            DMA((3,)),
            DMA((CHUNKS,)),
            DMA((8,)),
            DMA,
            DMA((4,)),
            DMA((4,)),
            DMA((4,)),
            DMA((36,)),
            DMA((36,)),
            DMA,
            DMA((4,)),
            DMA,
        ],
        compiler_params=pltpu.CompilerParams(
            collective_id=0, has_side_effects=True, vmem_limit_bytes=48 << 20
        ),
        name="harmonic_ilc",
    )(
        mode_values.reshape(1, 128),
        cycle_order.reshape(1, 256),
        bin_widths.reshape(1, 128),
        sky_maps.reshape(512, PIX),
        legendre,
    )
    return out.reshape(32, 2, 32, 128).transpose(0, 1, 3, 2)


def solution(mesh):
    return jax.shard_map(
        on_device,
        mesh=mesh,
        in_specs=(P("freq", "blk", None, None), P("blk", None, None), P(), P(), P()),
        out_specs=P(None, None, None, ("freq", "blk")),
        check_vma=False,
    )
```

time: 711 us -> 55.6 us (0.08); the launches traced: 698 us -> 55.4 us
  local copies, waits for them, and re-layouts: 324 us -> 2.96 us
  other arithmetic: 145 us -> 0 us
  blocking collectives: 125 us -> 0 us
  waiting for transfers between devices: 63.3 us -> 0 us
  Pallas kernels: 0 us -> 52.5 us
  matrix products: 26.6 us -> 0 us
  starting transfers between devices: 13.3 us -> 0 us
    another operation x22 -> x0, local copies, waits for them, and re-layouts: 148 us -> none  [the longest x17 147 us: on_device(): stacked = jnp.stack(results, axis=1)]
    another operation x12 -> x0, other arithmetic: 114 us -> none  [the longest x4 94.1 us: ilc_weights(): lower_factor = jnp.linalg.cholesky(loaded)]
    unnamed x15 -> x7, local copies, waits for them, and re-layouts: 73.4 us -> 2.96 us
    psum x1 -> x0, blocking collectives: 70.2 us -> none  [clean_band(): spectra = lax.psum(partial_value, ('freq', 'blk'))]
    all_to_all x4 -> x0, local copies, waits for them, and re-layouts: 67.7 us -> none  [the longest x2 52.1 us: on_device(): lax.all_to_all(lax.all_to_all(coeffs[None], 'freq', split_axis=4, concat_...]
    all_to_all x2 -> x0, waiting for transfers between devices: 63.3 us -> none  [the longest x1 59.1 us: on_device(): lax.all_to_all(lax.all_to_all(coeffs[None], 'freq', split_axis=4, concat_...]
    all_to_all x1 -> x0, blocking collectives: 55.1 us -> none  [on_device(): lax.all_to_all(coeffs[None], 'freq', split_axis=4, concat_axis=0, tiled=T...]
    pallas_call x0 -> x1, Pallas kernels: none -> 52.5 us  [on_device(): pl.pallas_call(kernel, out_shape=jax.ShapeDtypeStruct((64, 32, 128), F32)...]
  transfers between devices with their start and end apart: 2 -> 0, of which waited for: 2 -> 0; matrix products, arithmetic and copies ran while one was open for 1% -> 0% of each run, Pallas kernels for 0% -> 0%
where the time goes in v3:
time: 55.6 us; the launch traced here: 55.4 us
  Pallas kernels  52.5 us (94%)
  local copies, waits for them, and re-layouts  2.96 us (5%)
    pallas_call x1, Pallas kernels, on_device(): pl.pallas_call(kernel, out_shape=jax.ShapeDtypeStruct((64, 32, 128), F32)...  52.5 us
    unnamed x7, local copies, waits for them, and re-layouts  2.96 us

profile of v3, /device:TPU:1, one launch (start us, length us, event | category | flops | bytes accessed | tf_op | source)
XLA Modules:
  0.0 55.4 jit_solution(3021527993001166890)
XLA Ops:
  0.0 0.0 copy-start
  0.0 0.7 %copy-done = s32[256]{0:T(256)S(1)} copy-done((s32[256]{0:T(256)S(1)}, s32[256]{0:T(256)}, u32[]{:S(2)}) %copy-start) | copy-done | bytes 1048
  0.7 0.0 copy-start.1
  0.7 0.7 %copy-done.1 = s32[128]{0:T(128)S(1)} copy-done((s32[128]{0:T(128)S(1)}, s32[128]{0:T(128)}, u32[]{:S(2)}) %copy-start.1) | copy-done | bytes 536
  1.3 0.0 copy-start.2
  1.3 0.7 %copy-done.2 = s32[128]{0:T(128)S(1)} copy-done((s32[128]{0:T(128)S(1)}, s32[128]{0:T(128)}, u32[]{:S(2)}) %copy-start.2) | copy-done | bytes 536
  2.0 52.5 %harmonic_ilc.1 = f32[64,32,128]{2,1,0:T(8,128)S(1)} custom-call(s32[1,128]{1,0:T(1,128)S(1)} %bitcast.9, s32[1,256]{1,0:T(1,128)S(1)} %bitcast.8, s32[1,128]{1,0:T(1,128)S(1)} %bitcast.10, bf16[512,8192]{1,0:T(8,128)(2,1)} %bitcast.11, bf16[8,256,4096]{2,1,0:T(8,128)(2,1)} %leg_hbm.1), custom_call_target="tpu_custom_call" | custom-call | tf_op jit(solution)/shard_map/harmonic_ilc/pallas_call | solution.py:447
  54.5 1.0 %copy.7 = f32[32,2,128,32]{2,3,1,0:T(8,128)} copy(f32[32,2,128,32]{2,3,1,0:T(8,128)S(1)} %bitcast.7) | data formatting | bytes 2097152
Async XLA Ops:
  0.0 0.7 %copy-start = (s32[256]{0:T(256)S(1)}, s32[256]{0:T(256)}, u32[]{:S(2)}) copy-start(s32[256]{0:T(256)} %param.8) | copy-start | bytes 3076
  0.7 0.7 %copy-start.1 = (s32[128]{0:T(128)S(1)}, s32[128]{0:T(128)}, u32[]{:S(2)}) copy-start(s32[128]{0:T(128)} %param.7) | copy-start | bytes 1540
  1.3 0.7 %copy-start.2 = (s32[128]{0:T(128)S(1)}, s32[128]{0:T(128)}, u32[]{:S(2)}) copy-start(s32[128]{0:T(128)} %param.9) | copy-start | bytes 1540

commit v4 on v3

--- a/solution.py
+++ b/solution.py
@@ -10,7 +10,8 @@
 F32 = jnp.float32
 BF16 = jnp.bfloat16
 PIX = 8192
-CHUNKS = 16
+CHUNKS = 4
+TURNS = PIX // CHUNKS // 128
 WIDTH = PIX // CHUNKS
 PAIRS = [(i, j) for i in range(8) for j in range(i, 8)]
 PROWS = 40
@@ -57,8 +58,8 @@
 
 
 def turn(phase):
-    quadrant = (phase + PIX // 8) // (PIX // 4)
-    a = (phase - quadrant * (PIX // 4)).astype(F32) * jnp.float32(2.0 * math.pi / PIX)
+    quadrant = jnp.right_shift(phase + PIX // 8, 11)
+    a = (phase - jnp.left_shift(quadrant, 11)).astype(F32) * jnp.float32(2.0 * math.pi / PIX)
     a2 = a * a
     s = jnp.float32(1 / 362880)
     for coefficient in (-1 / 5040, 1 / 120, -1 / 6, 1.0):
@@ -67,11 +68,11 @@
     c = jnp.float32(-1 / 3628800)
     for coefficient in (1 / 40320, -1 / 720, 1 / 24, -1 / 2, 1.0):
         c = c * a2 + jnp.float32(coefficient)
-    odd = quadrant % 2 == 1
+    odd = (quadrant & 1) == 1
     cosine = jnp.where(odd, s, c)
     sine = jnp.where(odd, c, s)
-    cosine = jnp.where((quadrant + 1) % 4 >= 2, -cosine, cosine)
-    sine = jnp.where(quadrant % 4 >= 2, -sine, sine)
+    cosine = jnp.where(((quadrant + 1) & 2) == 2, -cosine, cosine)
+    sine = jnp.where((quadrant & 2) == 2, -sine, sine)
     return cosine, sine
 
 
@@ -88,8 +89,16 @@
         self.p = self.x * 16 + self.b
         self.partner = (self.x * 2 + 1 - self.c, self.b)
 
-    def device(self, x, y, z):
-        return (x * 2 + self.c, y * 4 + z)
+    def device(self, x, y, z, core=None):
+        return (x * 2 + (self.c if core is None else core), y * 4 + z)
+
+    def along(self, core=None):
+        x, y, z = self.x, self.y, self.z
+        return [
+            [self.device(x, y, wrap(z + d), core) for d in (2, 1, 3)],
+            [self.device(x, wrap(y + d), z, core) for d in (2, 1, 3)],
+            [self.device(wrap(x + d), y, z, core) for d in (2, 1, 3)],
+        ]
 
 
 def remote(src, dst, send, recv, device):
@@ -113,19 +122,19 @@
     m = modes[...]
     factor = jnp.float32(PIX ** (-0.5))
     high = lax.broadcasted_iota(jnp.int32, (64, 128), 0)
-    cosine, sine = turn((high * m) % 64 * 128)
+    cosine, sine = turn(jnp.left_shift((high * m) & 63, 7))
     tab_a[0] = cosine * factor
     tab_a[1] = sine * factor
     low = lax.broadcasted_iota(jnp.int32, (128, 128), 0)
-    cosine, sine = turn((low * m) % PIX)
+    cosine, sine = turn((low * m) & (PIX - 1))
     tab_b[0] = cosine
     tab_b[1] = sine
 
 
 def make_chunk(tab_a, tab_b, table, n):
-    for u in range(4):
-        ca = tab_a[0, pl.ds(n * 4 + u, 1), :]
-        sa = tab_a[1, pl.ds(n * 4 + u, 1), :]
+    for u in range(TURNS):
+        ca = tab_a[0, pl.ds(n * TURNS + u, 1), :]
+        sa = tab_a[1, pl.ds(n * TURNS + u, 1), :]
         lines = slice(u * 128, u * 128 + 128)
         table[lines, 0:128] = (tab_b[0] * ca - tab_b[1] * sa).astype(BF16)
         table[lines, 128:256] = (tab_b[1] * (-ca) - tab_b[0] * sa).astype(BF16)
@@ -195,19 +204,20 @@
             ].astype(BF16)
 
 
-def legendre_group(leg, left, coef, u):
+def legendre_group(leg, left, coef, fresh, u):
     lanes = pl.ds(pl.multiple_of(u * 256, 256), 256)
     for s in range(8):
-        out = jnp.dot(left[s], leg[u, s], preferred_element_type=F32)
-        coef[s, :, lanes] = out.astype(BF16)
-
-
-def spectra_group(coef, factors, sums, per_ell, onehot, total, u):
+        out = jnp.dot(left[s], leg[u, s], preferred_element_type=F32).astype(BF16)
+        fresh[s] = out
+        coef[s, :, lanes] = out
+
+
+def spectra_group(fresh, factors, sums, per_ell, onehot, total, u):
     for h in range(2):
-        lanes = pl.ds(pl.multiple_of(u * 256 + h * 128, 128), 128)
+        lanes = slice(h * 128, h * 128 + 128)
         acc = [None] * len(PAIRS)
         for s in range(8):
-            both = [coef[s, i * 16 : i * 16 + 16, lanes].astype(F32) for i in range(8)]
+            both = [fresh[s, i * 16 : i * 16 + 16, lanes].astype(F32) for i in range(8)]
             factor = factors[pl.ds(s, 1), :]
             for half in range(2):
                 values = [v[half * 8 : half * 8 + 8] for v in both]
@@ -225,62 +235,58 @@
     total[...] += split_dot(per_ell[...], onehot[:, group], NT)
 
 
-def legendre_spectra(leg_hbm, leg, sem, c, left, coef, factors, sums, per_ell, onehot, total):
+def legendre_spectra(
+    leg_hbm, leg, sem, c, left, coef, even, odd, factors, sums, per_ell, onehot, total
+):
     sums[...] = jnp.zeros_like(sums)
     total[...] = jnp.zeros_like(total)
-    legendre_copy(leg_hbm, leg, sem, c, 0).wait()
-    legendre_group(leg, left, coef, 0)
-
-    def step(u, _):
-        legendre_copy(leg_hbm, leg, sem, c, u + 1).wait()
-        legendre_group(leg, left, coef, u + 1)
-        spectra_group(coef, factors, sums, per_ell, onehot, total, u)
+    for u in range(8):
+        legendre_copy(leg_hbm, leg, sem, c, u).wait()
+    legendre_group(leg, left, coef, even, 0)
+
+    def step(v, _):
+        legendre_group(leg, left, coef, odd, v * 2 + 1)
+        spectra_group(even, factors, sums.at[0], per_ell.at[0], onehot, total, v * 2)
+        legendre_group(leg, left, coef, even, v * 2 + 2)
+        spectra_group(odd, factors, sums.at[1], per_ell.at[1], onehot, total, v * 2 + 1)
         return 0
 
-    lax.fori_loop(0, 7, step, 0)
-    spectra_group(coef, factors, sums, per_ell, onehot, total, 7)
+    lax.fori_loop(0, 3, step, 0)
+    legendre_group(leg, left, coef, odd, 7)
+    spectra_group(even, factors, sums.at[0], per_ell.at[0], onehot, total, 6)
+    spectra_group(odd, factors, sums.at[1], per_ell.at[1], onehot, total, 7)
 
 
 def sum_over_devices(me, part, got, send, recv):
-    x, y, z = me.x, me.y, me.z
-    peers = [
-        [me.device(x, y, wrap(z + d)) for d in (2, 1, 3)],
-        [me.device(x, wrap(y + d), z) for d in (2, 1, 3)],
-        [me.device(wrap(x + d), y, z) for d in (2, 1, 3)],
-    ]
-    started = []
+    near, far = me.along(), me.along(1 - me.c)
 
     def go(stage, index):
-        first, count = PARTS[index]
-        lines = pl.ds(first, count)
-        devices = peers[(stage + index) % 3] if stage < 3 else [me.partner]
-        copies = []
+        lines = pl.ds(*PARTS[index])
+        axis = (stage + index) % 3
+        devices = near[axis]
+        if stage == 2:
+            devices = near[axis] + far[axis] + [me.partner]
         for d, device in enumerate(devices):
-            n = (stage * 3 + index) * 3 + d
-            copies.append(
-                remote(
-                    part.at[stage, lines], got.at[stage, d, lines], send.at[n], recv.at[n], device
-                )
-            )
-            copies[-1].start()
-        started.extend(copies)
-        return copies
-
-    flights = [go(0, index) for index in range(3)]
-    for stage in range(4):
+            remote(
+                part.at[stage, lines], got.at[stage * 7 + d, lines], send,
+                recv.at[stage * 3 + index], device,
+            ).start()
+        return len(devices)
+
+    counts = [go(0, index) for index in range(3)]
+    for stage in range(3):
         later = []
         for index in range(3):
-            first, count = PARTS[index]
-            lines = pl.ds(first, count)
+            lines = pl.ds(*PARTS[index])
+            arrived = got.at[pl.ds(stage * 7, counts[index]), lines]
+            pltpu.make_async_copy(arrived, arrived, recv.at[stage * 3 + index]).wait()
             value = part[stage, lines, :]
-            for d, copy in enumerate(flights[index]):
-                copy.wait_recv()
-                value = value + got[stage, d, lines, :]
+            for d in range(counts[index]):
+                value = value + got[stage * 7 + d, lines, :]
             part[stage + 1, lines, :] = value
-            if stage < 3:
+            if stage < 2:
                 later.append(go(stage + 1, index))
-        flights = later
-    return started
+        counts = later
 
 
 def solve_bins(packed, matrix):
@@ -331,7 +337,7 @@
 def kernel(
     modes_hbm, order_hbm, widths_hbm, sky_hbm, leg_hbm, out_ref,
     modes, order, widths, xbuf, tab_a, tab_b, table, rows, sb1, rb1, perm, left, turned2, leg,
-    coef, sums, per_ell, onehot, factors, part, got, matrix, spread, turned, sb3, rb3,
+    coef, even, odd, sums, per_ell, onehot, factors, part, got, matrix, spread, turned, sb3, rb3,
     small_sem, sky_sem, leg_sem, send1, recv1, fsend, frecv, send2, recv2, send3, recv3, own,
 ):
     me = Place()
@@ -345,28 +351,31 @@
         copy.start()
     for n in range(CHUNKS):
         sky_copy(sky_hbm, xbuf, sky_sem, n).start()
-    for u in range(8):
-        legendre_copy(leg_hbm, leg, leg_sem, c, u).start()
     barrier = pltpu.get_barrier_semaphore()
     for i in range(4):
         for dy, dz in OFFSETS:
             if i or dy or dz:
                 device = me.device(wrap(x + i), wrap(me.y + dy), wrap(me.z + dz))
                 pl.semaphore_signal(barrier, device_id=device, device_id_type=MESH)
-    pl.semaphore_signal(barrier, device_id=me.partner, device_id_type=MESH)
+    for device in sum(me.along(1 - c), [me.partner]):
+        pl.semaphore_signal(barrier, device_id=device, device_id_type=MESH)
     for copy in small:
         copy.wait()
     make_tables(modes, tab_a, tab_b)
     fourier_rows(sky_hbm, xbuf, sky_sem, tab_a, tab_b, table, rows)
-    pl.semaphore_wait(barrier, 64)
-
-    for i in (2, 1, 3, 0):
+    for u in range(8):
+        legendre_copy(leg_hbm, leg, leg_sem, c, u).start()
+    pl.semaphore_wait(barrier, 73)
+
+    def swapped(i):
         xx = wrap(x + i)
         parts = [
-            rows[half, pl.ds(xx * 8 + k, 16, stride=32), :] for k in range(8) for half in range(2)
+            rows[half, pl.ds(xx * 8 + k, 16, stride=32), :].astype(BF16) for k in range(8) for half in range(2)
         ]
-        for g, block in enumerate(swap_blocks(parts, 8)):
-            sb1[xx * 16 + g] = block.astype(BF16)
+        return swap_blocks(parts, 8)
+
+    def send_group(i):
+        xx = wrap(x + i)
         for dy, dz in OFFSETS:
             if i or dy or dz:
                 yy, zz = wrap(me.y + dy), wrap(me.z + dz)
@@ -374,6 +383,16 @@
                     sb1.at[xx * 16 + yy * 4 + zz], rb1.at[c, me.p], send1, recv1.at[x],
                     me.device(xx, yy, zz),
                 ).start()
+
+    last = None
+    for i in (2, 1, 3, 0):
+        blocks = swapped(i)
+        if last is not None:
+            send_group(last)
+        for g, block in enumerate(blocks):
+            sb1[wrap(x + i) * 16 + g] = block
+        last = i
+    send_group(0)
     local = pltpu.make_async_copy(sb1.at[me.p], rb1.at[c, me.p], own)
     local.start()
     bin_columns(widths, c, onehot)
@@ -399,38 +418,43 @@
         order_channel(rb1, perm, left, turned2.at[1], 1 - c, g)
 
     legendre_spectra(
-        leg_hbm, leg, leg_sem, c, left, coef, factors, sums, per_ell, onehot, part.at[0]
+        leg_hbm, leg, leg_sem, c, left, coef, even, odd, factors, sums, per_ell, onehot, part.at[0]
     )
-    started = sum_over_devices(me, part, got, send2, recv2)
-    weights = solve_bins(part.at[4], matrix)
+    sum_over_devices(me, part, got, send2, recv2)
+    weights = solve_bins(part.at[3], matrix)
     spread[...] = split_dot(weights, onehot[...], NN)
 
-    def tile(n, _):
-        xx, yy = wrap(x + 1 + n // 4), wrap(me.y + 1 + n % 4)
-        for zz, block in enumerate(
-            weighted_tile(coef, spread, turned.at[lax.rem(n, 2)], xx * 4 + yy)
-        ):
-            sb3[xx * 16 + yy * 4 + zz] = block.astype(BF16)
-        for zz in range(4):
+    def tiles(xx, lines):
+        made = [
+            weighted_tile(coef, spread, turned.at[i], xx * 4 + yy) for i, yy in enumerate(lines)
+        ]
+        for yy, blocks in zip(lines, made):
+            for zz, block in enumerate(blocks):
+                sb3[xx * 16 + yy * 4 + zz] = block.astype(BF16)
+
+    def send_tile(xx, yy, places):
+        for zz in places:
             remote(
                 sb3.at[xx * 16 + yy * 4 + zz], rb3.at[me.p], send3, recv3.at[x],
                 me.device(xx, yy, zz),
             ).start()
+
+    def pair(n, _):
+        xx = wrap(x + 1 + n // 2)
+        lines = [wrap(me.y + 1 + n % 2 * 2), wrap(me.y + 2 + n % 2 * 2)]
+        tiles(xx, lines)
+        for yy in lines:
+            send_tile(xx, yy, range(4))
         return 0
 
-    lax.fori_loop(0, 15, tile, 0)
-    for zz, block in enumerate(weighted_tile(coef, spread, turned.at[1], x * 4 + me.y)):
-        sb3[x * 16 + me.y * 4 + zz] = block.astype(BF16)
-    for d in (2, 1, 3):
-        zz = wrap(me.z + d)
-        remote(
-            sb3.at[x * 16 + me.y * 4 + zz], rb3.at[me.p], send3, recv3.at[x],
-            me.device(x, me.y, zz),
-        ).start()
+    lax.fori_loop(0, 7, pair, 0)
+    lines = [wrap(me.y + 3), me.y]
+    tiles(x, lines)
+    send_tile(x, lines[0], range(4))
+    send_tile(x, me.y, [wrap(me.z + d) for d in (2, 1, 3)])
     local = pltpu.make_async_copy(sb3.at[me.p], rb3.at[me.p], own)
     local.start()
-    for copy in started:
-        copy.wait_send()
+    wait_blocks(got, send2, 13)
     for g in range(4):
         forward(c, g).wait_send()
     wait_blocks(sb1, send1, 63)
@@ -465,12 +489,14 @@
             VMEM((2, 2, 128, 128), F32),
             VMEM((8, 8, 256, 256), BF16),
             VMEM((8, 128, 2048), BF16),
-            VMEM((2, PROWS * 8, 128), F32),
-            VMEM((PROWS, 256), F32),
+            VMEM((8, 128, 256), BF16),
+            VMEM((8, 128, 256), BF16),
+            VMEM((2, 2, PROWS * 8, 128), F32),
+            VMEM((2, PROWS, 256), F32),
             VMEM((128, 2048), BF16),
             VMEM((8, 128), F32),
-            VMEM((5, PROWS, 128), F32),
-            VMEM((4, 3, PROWS, 128), F32),
+            VMEM((4, PROWS, 128), F32),
+            VMEM((21, PROWS, 128), F32),
             VMEM((8, 8, 128), F32),
             VMEM((8, 2048), F32),
             VMEM((2, 128, 128), F32),
@@ -483,8 +509,8 @@
             DMA((4,)),
             DMA((4,)),
             DMA((4,)),
-            DMA((36,)),
-            DMA((36,)),
+            DMA,
+            DMA((9,)),
             DMA,
             DMA((4,)),
             DMA,
@@ -494,11 +520,11 @@
         ),
         name="harmonic_ilc",
     )(
-        mode_values.reshape(1, 128),
-        cycle_order.reshape(1, 256),
-        bin_widths.reshape(1, 128),
-        sky_maps.reshape(512, PIX),
-        legendre,
+        pltpu.with_memory_space_constraint(mode_values.reshape(1, 128), pltpu.HBM),
+        pltpu.with_memory_space_constraint(cycle_order.reshape(1, 256), pltpu.HBM),
+        pltpu.with_memory_space_constraint(bin_widths.reshape(1, 128), pltpu.HBM),
+        pltpu.with_memory_space_constraint(sky_maps.reshape(512, PIX), pltpu.HBM),
+        pltpu.with_memory_space_constraint(legendre, pltpu.HBM),
     )
     return out.reshape(32, 2, 32, 128).transpose(0, 1, 3, 2)
 

time: 55.6 us -> 50 us (0.90)
  Pallas kernels: 52.5 us -> 49 us
  local copies, waits for them, and re-layouts: 2.96 us -> 0.97 us
    pallas_call x1, Pallas kernels: 52.5 us -> 49 us  [on_device(): pl.pallas_call(kernel, out_shape=jax.ShapeDtypeStruct((64, 32, 128), F32)...]
    unnamed x7 -> x1, local copies, waits for them, and re-layouts: 2.96 us -> 0.97 us
where the time goes in v4:
time: 50 us; the launch traced here: 49.9 us
  Pallas kernels  49 us (98%)
  local copies, waits for them, and re-layouts  0.97 us (2%)
    pallas_call x1, Pallas kernels, on_device(): pl.pallas_call(kernel, out_shape=jax.ShapeDtypeStruct((64, 32, 128), F32)...  49 us

profile of v4, /device:TPU:1, one launch (start us, length us, event | category | flops | bytes accessed | tf_op | source)
XLA Modules:
  0.0 49.9 jit_solution(17439206083054025835)
XLA Ops:
  0.0 49.0 %harmonic_ilc.1 = f32[64,32,128]{2,1,0:T(8,128)S(1)} custom-call(s32[1,128]{1,0:T(1,128)} %bitcast.10, s32[1,256]{1,0:T(1,128)} %bitcast.9, s32[1,128]{1,0:T(1,128)} %bitcast.11, bf16[512,8192]{1,0:T(8,128)(2,1)} %bitcast.8, bf16[8,256,4096]{2,1,0:T(8,128)(2,1)} %leg_hbm.1), custom_call_target="tpu_custom_call" | custom-call | tf_op jit(solution)/shard_map/harmonic_ilc/pallas_call | solution.py:471
  49.0 1.0 %copy.7 = f32[32,2,128,32]{2,3,1,0:T(8,128)} copy(f32[32,2,128,32]{2,3,1,0:T(8,128)S(1)} %bitcast.7) | data formatting | bytes 2097152

commit v5 on v4

--- a/solution.py
+++ b/solution.py
@@ -31,13 +31,13 @@
 
 
 def split_dot(a, b, dims):
-    hi = a.astype(BF16)
-    rest = a - hi.astype(F32)
-    mid = rest.astype(BF16)
-    low = (rest - mid.astype(F32)).astype(BF16)
-    out = lax.dot_general(low, b, dims, preferred_element_type=F32)
-    out += lax.dot_general(mid, b, dims, preferred_element_type=F32)
-    return out + lax.dot_general(hi, b, dims, preferred_element_type=F32)
+    count = a.shape[0]
+    hi = a.astype(BF16).astype(F32)
+    mid = (a - hi).astype(BF16).astype(F32)
+    low = a - hi - mid
+    parts = jnp.concatenate([low, mid, hi], axis=0).astype(BF16)
+    out = lax.dot_general(parts, b, dims, preferred_element_type=F32)
+    return out[:count] + out[count : 2 * count] + out[2 * count :]
 
 
 def swap_blocks(arrays, width):
@@ -204,33 +204,36 @@
             ].astype(BF16)
 
 
-def legendre_group(leg, left, coef, fresh, u):
+def legendre_group(leg, left, coef, fresh, u, slots=(0, 8)):
     lanes = pl.ds(pl.multiple_of(u * 256, 256), 256)
-    for s in range(8):
+    for j in range(slots[1]):
+        s = slots[0] + j
         out = jnp.dot(left[s], leg[u, s], preferred_element_type=F32).astype(BF16)
         fresh[s] = out
         coef[s, :, lanes] = out
 
 
-def spectra_group(fresh, factors, sums, per_ell, onehot, total, u):
-    for h in range(2):
-        lanes = slice(h * 128, h * 128 + 128)
-        acc = [None] * len(PAIRS)
-        for s in range(8):
-            both = [fresh[s, i * 16 : i * 16 + 16, lanes].astype(F32) for i in range(8)]
-            factor = factors[pl.ds(s, 1), :]
-            for half in range(2):
-                values = [v[half * 8 : half * 8 + 8] for v in both]
-                scaled = [v * factor for v in values]
-                for n, (i, j) in enumerate(PAIRS):
-                    product = scaled[i] * values[j]
-                    acc[n] = product if acc[n] is None else acc[n] + product
-        for n, value in enumerate(acc):
-            sums[h, n * 8 : n * 8 + 8, :] = value
-        line = sums[h, pl.ds(0, PROWS, stride=8), :]
-        for r in range(1, 8):
-            line = line + sums[h, pl.ds(r, PROWS, stride=8), :]
-        per_ell[:, h * 128 : h * 128 + 128] = line
+def spectra_tile(fresh, factors, sums, per_ell, h):
+    lanes = pl.ds(pl.multiple_of(h * 128, 128), 128)
+    acc = [None] * len(PAIRS)
+    for s in range(8):
+        both = [fresh[s, i * 16 : i * 16 + 16, lanes].astype(F32) for i in range(8)]
+        factor = factors[pl.ds(s, 1), :]
+        for half in range(2):
+            values = [v[half * 8 : half * 8 + 8] for v in both]
+            scaled = [v * factor for v in values]
+            for n, (i, j) in enumerate(PAIRS):
+                product = scaled[i] * values[j]
+                acc[n] = product if acc[n] is None else acc[n] + product
+    for n, value in enumerate(acc):
+        sums[n * 8 : n * 8 + 8, :] = value
+    line = sums[pl.ds(0, PROWS, stride=8), :]
+    for r in range(1, 8):
+        line = line + sums[pl.ds(r, PROWS, stride=8), :]
+    per_ell[:, lanes] = line
+
+
+def bin_group(per_ell, onehot, total, u):
     group = pl.ds(pl.multiple_of(u * 256, 256), 256)
     total[...] += split_dot(per_ell[...], onehot[:, group], NT)
 
@@ -244,17 +247,24 @@
         legendre_copy(leg_hbm, leg, sem, c, u).wait()
     legendre_group(leg, left, coef, even, 0)
 
+    def beside(make, made, u, last=False):
+        def half(h, _):
+            if not last:
+                legendre_group(leg, left, coef, make, u + 1, (h * 4, 4))
+            spectra_tile(made, factors, sums.at[0], per_ell.at[0], h)
+            return 0
+
+        lax.fori_loop(0, 2, half, 0)
+        bin_group(per_ell.at[0], onehot, total, u)
+
     def step(v, _):
-        legendre_group(leg, left, coef, odd, v * 2 + 1)
-        spectra_group(even, factors, sums.at[0], per_ell.at[0], onehot, total, v * 2)
-        legendre_group(leg, left, coef, even, v * 2 + 2)
-        spectra_group(odd, factors, sums.at[1], per_ell.at[1], onehot, total, v * 2 + 1)
+        beside(odd, even, v * 2)
+        beside(even, odd, v * 2 + 1)
         return 0
 
     lax.fori_loop(0, 3, step, 0)
-    legendre_group(leg, left, coef, odd, 7)
-    spectra_group(even, factors, sums.at[0], per_ell.at[0], onehot, total, 6)
-    spectra_group(odd, factors, sums.at[1], per_ell.at[1], onehot, total, 7)
+    beside(odd, even, 6)
+    beside(even, odd, 7, last=True)
 
 
 def sum_over_devices(me, part, got, send, recv):
@@ -424,11 +434,11 @@
     weights = solve_bins(part.at[3], matrix)
     spread[...] = split_dot(weights, onehot[...], NN)
 
-    def tiles(xx, lines):
+    def tiles(columns, yy):
         made = [
-            weighted_tile(coef, spread, turned.at[i], xx * 4 + yy) for i, yy in enumerate(lines)
+            weighted_tile(coef, spread, turned.at[i], xx * 4 + yy) for i, xx in enumerate(columns)
         ]
-        for yy, blocks in zip(lines, made):
+        for xx, blocks in zip(columns, made):
             for zz, block in enumerate(blocks):
                 sb3[xx * 16 + yy * 4 + zz] = block.astype(BF16)
 
@@ -440,17 +450,17 @@
             ).start()
 
     def pair(n, _):
-        xx = wrap(x + 1 + n // 2)
-        lines = [wrap(me.y + 1 + n % 2 * 2), wrap(me.y + 2 + n % 2 * 2)]
-        tiles(xx, lines)
-        for yy in lines:
+        columns = [wrap(x + 1 + n // 4), wrap(x + 3 + n // 4)]
+        yy = wrap(me.y + 1 + n % 4)
+        tiles(columns, yy)
+        for xx in columns:
             send_tile(xx, yy, range(4))
         return 0
 
     lax.fori_loop(0, 7, pair, 0)
-    lines = [wrap(me.y + 3), me.y]
-    tiles(x, lines)
-    send_tile(x, lines[0], range(4))
+    columns = [wrap(x + 2), x]
+    tiles(columns, me.y)
+    send_tile(columns[0], me.y, range(4))
     send_tile(x, me.y, [wrap(me.z + d) for d in (2, 1, 3)])
     local = pltpu.make_async_copy(sb3.at[me.p], rb3.at[me.p], own)
     local.start()
@@ -459,7 +469,7 @@
         forward(c, g).wait_send()
     wait_blocks(sb1, send1, 63)
     local.wait()
-    for i in (3, 2, 1, 0):
+    for i in (3, 1, 2, 0):
         g = wrap(x + i)
         wait_blocks(rb3, recv3.at[g], 16 if i else 15)
         output_group(rb3, out_ref, g)
@@ -491,8 +501,8 @@
             VMEM((8, 128, 2048), BF16),
             VMEM((8, 128, 256), BF16),
             VMEM((8, 128, 256), BF16),
-            VMEM((2, 2, PROWS * 8, 128), F32),
-            VMEM((2, PROWS, 256), F32),
+            VMEM((1, PROWS * 8, 128), F32),
+            VMEM((1, PROWS, 256), F32),
             VMEM((128, 2048), BF16),
             VMEM((8, 128), F32),
             VMEM((4, PROWS, 128), F32),

time: 50 us -> 49.2 us (0.984)
  Pallas kernels: 49 us -> 47.9 us
    pallas_call x1, Pallas kernels: 49 us -> 47.9 us  [on_device(): pl.pallas_call(kernel, out_shape=jax.ShapeDtypeStruct((64, 32, 128), F32)...]
where the time goes in v5:
time: 49.2 us; the launch traced here: 48.8 us
  Pallas kernels  47.9 us (97%)
  local copies, waits for them, and re-layouts  0.97 us (2%)
    pallas_call x1, Pallas kernels, on_device(): pl.pallas_call(kernel, out_shape=jax.ShapeDtypeStruct((64, 32, 128), F32)...  47.9 us

profile of v5, /device:TPU:1, one launch (start us, length us, event | category | flops | bytes accessed | tf_op | source)
XLA Modules:
  0.0 48.8 jit_solution(14152088883789865278)
XLA Ops:
  0.0 47.9 %harmonic_ilc.1 = f32[64,32,128]{2,1,0:T(8,128)S(1)} custom-call(s32[1,128]{1,0:T(1,128)} %bitcast.10, s32[1,256]{1,0:T(1,128)} %bitcast.9, s32[1,128]{1,0:T(1,128)} %bitcast.11, bf16[512,8192]{1,0:T(8,128)(2,1)} %bitcast.8, bf16[8,256,4096]{2,1,0:T(8,128)(2,1)} %leg_hbm.1), custom_call_target="tpu_custom_call" | custom-call | tf_op jit(solution)/shard_map/harmonic_ilc/pallas_call | solution.py:481
  47.9 1.0 %copy.7 = f32[32,2,128,32]{2,3,1,0:T(8,128)} copy(f32[32,2,128,32]{2,3,1,0:T(8,128)S(1)} %bitcast.7) | data formatting | bytes 2097152

commit v6 on v5

--- a/solution.py
+++ b/solution.py
@@ -15,7 +15,7 @@
 WIDTH = PIX // CHUNKS
 PAIRS = [(i, j) for i in range(8) for j in range(i, 8)]
 PROWS = 40
-PARTS = [(0, 16), (16, 16), (32, 8)]
+PARTS = [(0, 16), (16, 24)]
 MESH = pl.DeviceIdType.MESH
 VMEM = pltpu.VMEM
 DMA = pltpu.SemaphoreType.DMA
@@ -269,32 +269,33 @@
 
 def sum_over_devices(me, part, got, send, recv):
     near, far = me.along(), me.along(1 - me.c)
+    groups = [
+        [me.device(me.x, wrap(me.y + dy), wrap(me.z + dz)) for dy, dz in OFFSETS if dy or dz],
+        near[2] + far[2] + [me.partner],
+    ]
 
     def go(stage, index):
         lines = pl.ds(*PARTS[index])
-        axis = (stage + index) % 3
-        devices = near[axis]
-        if stage == 2:
-            devices = near[axis] + far[axis] + [me.partner]
+        devices = groups[(stage + index) % 2]
         for d, device in enumerate(devices):
             remote(
-                part.at[stage, lines], got.at[stage * 7 + d, lines], send,
-                recv.at[stage * 3 + index], device,
+                part.at[stage, lines], got.at[stage * 15 + d, lines], send,
+                recv.at[stage * 2 + index], device,
             ).start()
         return len(devices)
 
-    counts = [go(0, index) for index in range(3)]
-    for stage in range(3):
+    counts = [go(0, index) for index in range(2)]
+    for stage in range(2):
         later = []
-        for index in range(3):
+        for index in range(2):
             lines = pl.ds(*PARTS[index])
-            arrived = got.at[pl.ds(stage * 7, counts[index]), lines]
-            pltpu.make_async_copy(arrived, arrived, recv.at[stage * 3 + index]).wait()
+            arrived = got.at[pl.ds(stage * 15, counts[index]), lines]
+            pltpu.make_async_copy(arrived, arrived, recv.at[stage * 2 + index]).wait()
             value = part[stage, lines, :]
             for d in range(counts[index]):
-                value = value + got[stage * 7 + d, lines, :]
+                value = value + got[stage * 15 + d, lines, :]
             part[stage + 1, lines, :] = value
-            if stage < 2:
+            if stage < 1:
                 later.append(go(stage + 1, index))
         counts = later
 
@@ -421,7 +422,8 @@
         g = wrap(x + i)
         wait_blocks(rb1.at[c], recv1.at[g], 16 if i else 15)
         forward(c, g).start()
-        order_channel(rb1, perm, left, turned2.at[0], c, g)
+    for i in (2, 1, 3, 0):
+        order_channel(rb1, perm, left, turned2.at[0], c, wrap(x + i))
     for i in (2, 1, 3, 0):
         g = wrap(x + i)
         forward(1 - c, g).wait_recv()
@@ -431,7 +433,7 @@
         leg_hbm, leg, leg_sem, c, left, coef, even, odd, factors, sums, per_ell, onehot, part.at[0]
     )
     sum_over_devices(me, part, got, send2, recv2)
-    weights = solve_bins(part.at[3], matrix)
+    weights = solve_bins(part.at[2], matrix)
     spread[...] = split_dot(weights, onehot[...], NN)
 
     def tiles(columns, yy):
@@ -464,7 +466,7 @@
     send_tile(x, me.y, [wrap(me.z + d) for d in (2, 1, 3)])
     local = pltpu.make_async_copy(sb3.at[me.p], rb3.at[me.p], own)
     local.start()
-    wait_blocks(got, send2, 13)
+    wait_blocks(got, send2, 22)
     for g in range(4):
         forward(c, g).wait_send()
     wait_blocks(sb1, send1, 63)
@@ -506,7 +508,7 @@
             VMEM((128, 2048), BF16),
             VMEM((8, 128), F32),
             VMEM((4, PROWS, 128), F32),
-            VMEM((21, PROWS, 128), F32),
+            VMEM((30, PROWS, 128), F32),
             VMEM((8, 8, 128), F32),
             VMEM((8, 2048), F32),
             VMEM((2, 128, 128), F32),

time: 49.2 us -> 47.8 us (0.972)
  Pallas kernels: 47.9 us -> 46.3 us
    pallas_call x1, Pallas kernels: 47.9 us -> 46.3 us  [on_device(): pl.pallas_call(kernel, out_shape=jax.ShapeDtypeStruct((64, 32, 128), F32)...]
where the time goes in v6:
time: 47.8 us; the launch traced here: 47.3 us
  Pallas kernels  46.3 us (97%)
  local copies, waits for them, and re-layouts  0.97 us (2%)
    pallas_call x1, Pallas kernels, on_device(): pl.pallas_call(kernel, out_shape=jax.ShapeDtypeStruct((64, 32, 128), F32)...  46.3 us
    unnamed x1, local copies, waits for them, and re-layouts  0.97 us

profile of v6, /device:TPU:1, one launch (start us, length us, event | category | flops | bytes accessed | tf_op | source)
XLA Modules:
  0.0 47.3 jit_solution(140872048738958718)
XLA Ops:
  0.0 46.3 %harmonic_ilc.1 = f32[64,32,128]{2,1,0:T(8,128)S(1)} custom-call(s32[1,128]{1,0:T(1,128)} %bitcast.10, s32[1,256]{1,0:T(1,128)} %bitcast.9, s32[1,128]{1,0:T(1,128)} %bitcast.11, bf16[512,8192]{1,0:T(8,128)(2,1)} %bitcast.8, bf16[8,256,4096]{2,1,0:T(8,128)(2,1)} %leg_hbm.1), custom_call_target="tpu_custom_call" | custom-call | tf_op jit(solution)/shard_map/harmonic_ilc/pallas_call | solution.py:483
  46.3 1.0 %copy.7 = f32[32,2,128,32]{2,3,1,0:T(8,128)} copy(f32[32,2,128,32]{2,3,1,0:T(8,128)S(1)} %bitcast.7) | data formatting | bytes 2097152
